TPU v7x, 128 devices: a whole 4x4x4 slice. The times are simulated.
128 devices in a mesh: rows: 32 (over x, y, z_lo), feat: 4 (over z_hi, core).
Axes of the slice: x: 4, y: 4, z: 4 (z_hi: 2, z_lo: 2; z = z_hi * 2 + z_lo), core: 2. Of those that a mesh axis runs over, the one named last changes fastest.
Arguments:
- node_feats: bfloat16 [256, 131072], P('feat', 'rows'), may hold values from -6 to 6
- tile_vals: bfloat16 [1024, 16, 128, 128], P('rows'), may hold values from -0.125 to 0.125
- tile_cols: int32 [1024, 16], P('rows'), may hold values from 0 to 1023, as said below
- weight: bfloat16 [256, 256], P(None, 'feat'), may hold values from -0.375 to 0.375
- bias_vec: float32 [256], P('feat'), may hold values from -3 to 3
- grad_out: bfloat16 [256, 131072], P('feat', 'rows'), may hold values from -6 to 6
Outputs:
- activated: bfloat16 [256, 131072], P('feat', 'rows')
- grad_feats: float32 [256, 131072], P('feat', 'rows')
- grad_weight: float32 [256, 256], P(None, 'feat')
- grad_bias: float32 [256], P('feat')
Inputs may be any that keep to these rules, and one draw needn't show every extreme that they name: `tile_cols`: among the tiles of one device's 32 blocks of rows, the column blocks held by any one owner (blocks o * 32 to o * 32 + 31) are at most 16 distinct ones and at least one; on every device some owner reaches 16.
All inputs are finite; a program needn't handle non-finite values.
Results may differ from a plain program's by a relative error of at most 0.007.
Values may be sent and summed in bfloat16 or wider, within the bound.
No kernel may reach another device: no remote copies, remote signals or barrier semaphores. Data moves between devices by JAX's collectives and lax.ppermute only.
A program may use at most 256 MiB of HBM per device.

v0:
```python
import functools

import jax
import jax.numpy as jnp
from jax import lax
from jax.experimental import pallas as pl
from jax.experimental.pallas import tpu as pltpu
from jax.sharding import PartitionSpec as P

CAP = 16
BATCH = 8
TB = 128
MIB = 1 << 20
SIDE = 4
PLANES = 2
NEAR = SIDE * PLANES
PART = NEAR * CAP


def row_perm(dx, dy, dz):
    def index(x, y, z):
        return ((x % SIDE) * SIDE + y % SIDE) * PLANES + z % PLANES

    return [
        (index(x, y, z), index(x + dx, y + dy, z + dz))
        for x in range(SIDE)
        for y in range(SIDE)
        for z in range(PLANES)
    ]


def shift(v, near_axis, near, far):
    return lax.ppermute(v, "rows", row_perm(near, far, 0) if near_axis == 0 else row_perm(far, near, 0))


def pack_kernel(asked_ref, *refs):
    outs = refs[-6:]
    half = refs[0].shape[0] // PLANES
    for h in range(2):
        own, plus, minus = outs[3 * h : 3 * h + 3]
        near, plus_near, minus_near, upper, lower = refs[5 * h : 5 * h + 5]
        parts = [pl.ds(plane * half, half) for plane in range(PLANES)]
        sources = [held.at[rows] for held in (near, plus_near) for rows in parts]
        sources += [upper, lower] + [minus_near.at[rows] for rows in parts]
        for far in range(SIDE):
            for p in range(NEAR):
                source = sources[p]
                for k in range(CAP):
                    at = pl.multiple_of(asked_ref[h, far, p, k] * TB, TB)
                    place = p * CAP + k
                    if far == 2:
                        out, place = (plus, PART + place) if place < PART // 2 else (minus, PART // 2 + place)
                    else:
                        out = (own, plus, None, minus)[far]
                    out[place] = source[:, pl.ds(at, TB)]


def pack(asked, sources):
    half = sources[0].shape[0] // 2
    vmem = pl.BlockSpec(memory_space=pltpu.VMEM)
    out = pl.pallas_call(
        pack_kernel,
        out_shape=[
            jax.ShapeDtypeStruct((n, half, TB), sources[0].dtype) for n in (PART, PART * 3 // 2, PART * 3 // 2) * 2
        ],
        in_specs=[pl.BlockSpec(memory_space=pltpu.SMEM)] + [vmem] * len(sources),
        out_specs=[vmem] * 6,
        compiler_params=pltpu.CompilerParams(vmem_limit_bytes=40 * MIB),
        name="pack",
    )(asked, *sources)
    return out[:3], out[3:]


def exchange(messages, sign, side=None):
    first = [
        [shift(plus, h, 0, sign), shift(minus, h, 0, -sign)] for h, (_, plus, minus) in enumerate(messages)
    ]
    if side is not None:
        first, side = lax.optimization_barrier((first, side))
    second = [
        [shift(plus[PART:], h, 0, sign), shift(minus[PART:], h, 0, -sign)] for h, (plus, minus) in enumerate(first)
    ]
    return [[messages[h][0], *first[h], *second[h]] for h in range(2)], side


LAID = ((0, PART), (PART, PART), (3 * PART, PART), (2 * PART, PART // 2), (2 * PART + PART // 2, PART // 2))


def aggregate_kernel(slot_a_ref, slot_b_ref, *refs):
    n = len(LAID)
    got, (vals_ref, out_ref, a_ref, b_ref, sem) = refs[: 2 * n], refs[2 * n :]
    step = pl.program_id(0)
    per, slots = vals_ref.shape[:2]

    @pl.when(step == 0)
    def _():
        copies = []
        for j, held in enumerate((a_ref, b_ref)):
            for k, (at, size) in enumerate(LAID):
                copies.append(
                    pltpu.make_async_copy(
                        got[j * n + k].at[pl.ds(0, size)], held.at[pl.ds(at, size)], sem.at[j * n + k]
                    )
                )
        for copy in copies:
            copy.start()
        for copy in copies:
            copy.wait()

    for j in range(per):
        i = step * per + j
        a = jnp.concatenate([a_ref[slot_a_ref[i, s]] for s in range(slots)], axis=1)
        b = jnp.concatenate([b_ref[slot_b_ref[i, s]] for s in range(slots)], axis=1)
        tiles = jnp.concatenate([vals_ref[j, s] for s in range(slots)], axis=1)
        out = lax.dot_general(
            jnp.concatenate([a, b], axis=0), tiles, (((1,), (1,)), ((), ())), preferred_element_type=jnp.float32
        )
        out_ref[:, j * TB : (j + 1) * TB] = out.astype(out_ref.dtype)


def aggregate(slot_a, slot_b, got_a, got_b, vals):
    blocks, slots = slot_a.shape
    half = got_a[0].shape[1]
    per = 4
    return pl.pallas_call(
        aggregate_kernel,
        out_shape=jax.ShapeDtypeStruct((2 * half, blocks * TB), jnp.bfloat16),
        grid_spec=pltpu.PrefetchScalarGridSpec(
            num_scalar_prefetch=2,
            grid=(blocks // per,),
            in_specs=[pl.BlockSpec(memory_space=pltpu.HBM)] * (2 * len(LAID))
            + [pl.BlockSpec((per, slots, TB, TB), lambda i, a, b: (i, 0, 0, 0))],
            out_specs=pl.BlockSpec((2 * half, per * TB), lambda i, a, b: (0, i)),
            scratch_shapes=[pltpu.VMEM((SIDE * PART, half, TB), jnp.bfloat16)] * 2
            + [pltpu.SemaphoreType.DMA((2 * len(LAID),))],
        ),
        compiler_params=pltpu.CompilerParams(vmem_limit_bytes=40 * MIB),
        name="aggregate",
    )(slot_a, slot_b, *got_a, *got_b, vals)


def spread_kernel(slot_a_ref, slot_b_ref, mix_ref, vals_ref, *refs):
    outs, (a_ref, b_ref) = refs[:6], refs[6:]
    step = pl.program_id(0)
    per, slots = vals_ref.shape[:2]
    half = a_ref.shape[1]

    @pl.when(step == 0)
    def _():
        a_ref[...] = jnp.zeros_like(a_ref)
        b_ref[...] = jnp.zeros_like(b_ref)

    for j in range(per):
        i = step * per + j
        mix = mix_ref[:, j * TB : (j + 1) * TB]
        for s in range(slots):
            term = jnp.dot(mix, vals_ref[j, s], preferred_element_type=jnp.float32)
            a_ref[slot_a_ref[i, s]] += term[:half]
            b_ref[slot_b_ref[i, s]] += term[half:]

    @pl.when(step == pl.num_programs(0) - 1)
    def _():
        for j, held in enumerate((a_ref, b_ref)):
            own, plus, minus = outs[3 * j : 3 * j + 3]
            for out, to, (at, size) in zip((own, plus, minus, plus, minus), (0, 0, 0, PART, PART), LAID):
                out[pl.ds(to, size)] = held[pl.ds(at, size)].astype(jnp.bfloat16)


def spread(slot_a, slot_b, mix, vals):
    blocks, slots = slot_a.shape
    half = mix.shape[0] // 2
    per = 4
    out = pl.pallas_call(
        spread_kernel,
        out_shape=[jax.ShapeDtypeStruct((n, half, TB), jnp.bfloat16) for n in (PART, PART * 3 // 2, PART * 3 // 2) * 2],
        grid_spec=pltpu.PrefetchScalarGridSpec(
            num_scalar_prefetch=2,
            grid=(blocks // per,),
            in_specs=[
                pl.BlockSpec((2 * half, per * TB), lambda i, a, b: (0, i)),
                pl.BlockSpec((per, slots, TB, TB), lambda i, a, b: (i, 0, 0, 0)),
            ],
            out_specs=[
                pl.BlockSpec((n, half, TB), lambda i, a, b: (0, 0, 0), pipeline_mode=pl.Buffered(1))
                for n in (PART, PART * 3 // 2, PART * 3 // 2) * 2
            ],
            scratch_shapes=[pltpu.VMEM((SIDE * PART, half, TB), jnp.float32)] * 2,
        ),
        compiler_params=pltpu.CompilerParams(vmem_limit_bytes=48 * MIB),
        name="spread",
    )(slot_a, slot_b, mix, vals)
    return out[:3], out[3:]


def fold_kernel(asked_ref, *refs):
    n = len(LAID)
    got, outs, (acc_ref,) = refs[: 2 * n], refs[2 * n : -1], refs[-1:]
    p = pl.program_id(0)
    for h in range(2):
        acc_ref[...] = jnp.zeros_like(acc_ref)

        def add(held, far):
            for start in range(CAP - BATCH, -1, -BATCH):
                at = [
                    pl.ds(pl.multiple_of(asked_ref[h, far, p, k] * TB, TB), TB) for k in range(start, start + BATCH)
                ]
                sums = [acc_ref[:, to] + held[start + j].astype(jnp.float32) for j, to in enumerate(at)]
                for to, total in reversed(list(zip(at, sums))):
                    acc_ref[:, to] = total

        own, plus, minus, upper, lower = got[h * n : h * n + n]
        for held, far in ((own, 0), (plus, 1), (minus, 3)):
            add(held, far)
        pl.when(p < NEAR // 2)(functools.partial(add, upper, 2))
        pl.when(p >= NEAR // 2)(functools.partial(add, lower, 2))
        for plane in range(PLANES):
            own, plus, minus = outs[(h * PLANES + plane) * 3 :][:3]
            half = own.shape[0]

            @pl.when(p == plane)
            def _():
                own[...] = acc_ref[...]

            @pl.when(p == PLANES + plane)
            def _():
                plus[:half] = acc_ref[...].astype(plus.dtype)

            @pl.when(p == 2 * PLANES + plane)
            def _():
                plus[half:] = acc_ref[: half // 2].astype(plus.dtype)
                minus[half:] = acc_ref[half // 2 :].astype(minus.dtype)

            @pl.when(p == 3 * PLANES + plane)
            def _():
                minus[:half] = acc_ref[...].astype(minus.dtype)


def fold(asked, got, width):
    half = got[0].shape[1]
    block = (CAP, half, TB)
    specs = [pl.BlockSpec(block, lambda p, a: (p, 0, 0))] * 3 + [
        pl.BlockSpec(block, lambda p, a: (jnp.minimum(p, NEAR // 2 - 1), 0, 0)),
        pl.BlockSpec(block, lambda p, a: (jnp.maximum(p - NEAR // 2, 0), 0, 0)),
    ]
    out = pl.pallas_call(
        fold_kernel,
        out_shape=[
            jax.ShapeDtypeStruct((half, width), jnp.float32),
            jax.ShapeDtypeStruct((half * 3 // 2, width), jnp.bfloat16),
            jax.ShapeDtypeStruct((half * 3 // 2, width), jnp.bfloat16),
        ]
        * (2 * PLANES),
        grid_spec=pltpu.PrefetchScalarGridSpec(
            num_scalar_prefetch=1,
            grid=(NEAR,),
            in_specs=specs * 2,
            out_specs=[
                pl.BlockSpec((rows, width), lambda p, a: (0, 0), pipeline_mode=pl.Buffered(1))
                for rows in (half, half * 3 // 2, half * 3 // 2) * (2 * PLANES)
            ],
            scratch_shapes=[pltpu.VMEM((half, width), jnp.float32)],
        ),
        compiler_params=pltpu.CompilerParams(vmem_limit_bytes=40 * MIB),
        name="fold",
    )(asked, *got)
    return [[out[(h * PLANES + plane) * 3 :][:3] for plane in range(PLANES)] for h in range(2)]


def line_sum(folded, plane, side=None):
    first = [
        [shift(parts[plane][1], h, 1, 0), shift(parts[plane][2], h, -1, 0)] for h, parts in enumerate(folded)
    ]
    if side is not None:
        first, side = lax.optimization_barrier((first, side))
    sums = []
    for h, (plus, minus) in enumerate(first):
        own = folded[h][plane][0]
        half = own.shape[0]
        passed = [shift(plus[half:], h, 1, 0), shift(minus[half:], h, -1, 0)]
        total = own + plus[:half].astype(jnp.float32) + minus[:half].astype(jnp.float32)
        sums.append(total + jnp.concatenate(passed, axis=0).astype(jnp.float32))
    return jnp.concatenate(sums, axis=0), side


def requests(cols, owners, blocks):
    flat = cols.reshape(-1)
    hit = flat[:, None] == jnp.arange(owners * blocks, dtype=jnp.int32)[None, :]
    named = jnp.any(hit, axis=0).reshape(owners, blocks)
    before = jnp.arange(blocks)[:, None] < jnp.arange(blocks)[None, :]
    rank = jnp.sum(jnp.where(named[:, :, None] & before[None], 1, 0), axis=1).astype(jnp.int32)
    at = named[:, None, :] & (rank[:, None, :] == jnp.arange(CAP, dtype=jnp.int32)[None, :, None])
    wanted = jnp.sum(jnp.where(at, jnp.arange(blocks, dtype=jnp.int32)[None, None, :], 0), axis=2)
    place = jnp.sum(jnp.where(hit, rank.reshape(1, -1), 0), axis=1).astype(jnp.int32)
    return wanted.astype(jnp.int32), place.reshape(cols.shape)


def relative(table, x, y, z):
    for axis, (mine, size) in enumerate(((x, SIDE), (y, SIDE), (z, PLANES))):
        doubled = jnp.concatenate([table, table], axis=axis)
        table = lax.dynamic_slice_in_dim(doubled, mine, size, axis=axis)
    return table


def from_feat(v, step):
    return lax.ppermute(v, "feat", [(i, i ^ step) for i in range(4)])


def every_feat(v):
    two = from_feat(v, 2)
    return v, from_feat(v, 1), two, from_feat(two, 1)


def row_swap(v, dx, dy, dz):
    pairs = [
        ((x * SIDE + y) * PLANES + z, ((x ^ dx) * SIDE + (y ^ dy)) * PLANES + (z ^ dz))
        for x in range(SIDE)
        for y in range(SIDE)
        for z in range(PLANES)
    ]
    return v + lax.ppermute(v, "rows", pairs)


def blocks_by_feat(v, mine):
    size = v.shape[0] // 4
    return jnp.concatenate([lax.dynamic_slice_in_dim(v, (mine ^ j) * size, size, axis=0) for j in range(4)], axis=0)


def on_device(node_feats, tile_vals, tile_cols, weight, bias_vec, grad_out):
    feat_loc, width = node_feats.shape
    own_blocks = tile_cols.shape[0]
    half = feat_loc // 2
    me = lax.axis_index("rows")
    x, y, z = me // NEAR, (me // PLANES) % SIDE, me % PLANES
    mine = lax.axis_index("feat")

    other = lax.ppermute(node_feats, "rows", row_perm(0, 0, 1))
    wanted, place = requests(tile_cols, SIDE * NEAR, own_blocks)
    owner = tile_cols // own_blocks
    dx, dy = (owner // NEAR - x) % SIDE, ((owner // PLANES) % SIDE - y) % SIDE
    dz = (owner - z) % PLANES
    slots = [
        ((far * SIDE + near) * PLANES + dz) * CAP + place for near, far in ((dx, dy), (dy, dx))
    ]
    by_place = relative(wanted.reshape(SIDE, SIDE, PLANES, CAP), x, y, z)
    tables = [by_place.transpose(1, 0, 2, 3).reshape(SIDE, NEAR, CAP), by_place.reshape(SIDE, NEAR, CAP)]
    shards = []
    for h in range(2):
        rows = slice(h * half, (h + 1) * half)
        aside = jnp.pad(tables[1 - h].reshape(SIDE, PART).astype(jnp.bfloat16), ((0, feat_loc - SIDE), (0, 0)))
        both = jnp.concatenate([node_feats[rows], other[rows]], axis=0)
        shards.append(jnp.concatenate([both, aside], axis=1))
    first = [[shift(shards[h], h, -1, 0), shift(shards[h], h, 1, 0)] for h in range(2)]
    second = [[shift(first[h][0][:half], h, -1, 0), shift(first[h][1][half:], h, 1, 0)] for h in range(2)]
    lines = [v for h in range(2) for v in (shards[h], *first[h], *second[h])]
    asked = []
    for h in range(2):
        (plus, minus), (upper, _) = first[1 - h], second[1 - h]
        heard = [v[far, width:].astype(jnp.int32) for far, v in ((1, minus), (2, upper), (3, plus))]
        asked.append(jnp.stack([tables[h][0]] + [v.reshape(NEAR, CAP) for v in heard]))
    asked = jnp.stack(asked)
    lines, weight, bias_vec, grad_out = lax.optimization_barrier((lines, weight, bias_vec, grad_out))

    wide = jnp.concatenate([weight.astype(jnp.float32), jnp.broadcast_to(bias_vec[None], (8, feat_loc))], axis=0)
    wide = jnp.concatenate(every_feat(wide), axis=1)
    weight_all = blocks_by_feat(wide[: weight.shape[0]].astype(jnp.bfloat16), mine)
    bias_all = wide[weight.shape[0]]
    grad_out_all = jnp.concatenate(every_feat(grad_out), axis=0)

    got, _ = exchange(pack(asked, lines), -1)
    aggregated = aggregate(*slots, *got, tile_vals)
    agg_all = jnp.concatenate(every_feat(aggregated), axis=0)
    preact = (
        lax.dot_general(weight_all, agg_all, (((0,), (0,)), ((), ())), preferred_element_type=jnp.float32)
        + bias_all[:, None]
    )
    sigma = jax.nn.sigmoid(preact)
    activated = (preact[:feat_loc] * sigma[:feat_loc]).astype(jnp.bfloat16)
    grad_pre = (grad_out_all.astype(jnp.float32) * sigma * (1.0 + preact * (1.0 - sigma))).astype(jnp.bfloat16)
    back_mix = jnp.dot(weight_all[:feat_loc], grad_pre, preferred_element_type=jnp.float32).astype(jnp.bfloat16)

    terms = spread(*slots, back_mix, tile_vals)

    own_grad = grad_pre[:feat_loc]
    weight_part = lax.dot_general(own_grad, agg_all, (((1,), (1,)), ((), ())), preferred_element_type=jnp.float32)
    bias_part = jnp.sum(own_grad.astype(jnp.float32), axis=1)
    bias_rows = jnp.broadcast_to(jnp.pad(bias_part, (0, weight.shape[0] - feat_loc))[None], (8, weight.shape[0]))
    parts = jnp.concatenate([weight_part, bias_rows], axis=0)
    for step in ((0, 0, 1), (0, 1, 0)):
        parts = row_swap(parts, *step)

    back, parts = exchange(terms, 1, parts)
    parts = row_swap(parts, 0, 2, 0)
    back, parts = lax.optimization_barrier((back, parts))
    folded = fold(asked, back[0] + back[1], width)
    passed, parts = line_sum(folded, 1, row_swap(parts, 1, 0, 0))
    passed, parts = passed.astype(jnp.bfloat16), row_swap(parts, 2, 0, 0)
    passed, folded, parts = lax.optimization_barrier((passed, folded, parts))
    arrived = lax.ppermute(passed, "rows", row_perm(0, 0, 1))
    grad_feats = line_sum(folded, 0)[0] + arrived.astype(jnp.float32)
    grad_bias = parts[feat_loc, :feat_loc]
    grad_weight = blocks_by_feat(parts[:feat_loc].T, mine)
    return (activated, grad_feats, grad_weight, grad_bias)


def solution(mesh):
    placed = (
        P("feat", "rows"),
        P("rows", None, None, None),
        P("rows", None),
        P(None, "feat"),
        P("feat"),
        P("feat", "rows"),
    )
    return jax.shard_map(
        on_device,
        mesh=mesh,
        in_specs=placed,
        out_specs=(P("feat", "rows"), P("feat", "rows"), P(None, "feat"), P("feat")),
        check_vma=False,
    )
```

profile of v0, /device:TPU:24, one launch (start us, length us, event | category | flops | bytes accessed | tf_op | source)
XLA Modules:
  0.0 282.3 jit_solution(6213446040999090376)
XLA Ops:
  6.8 7.9 %collective-permute-done = bf16[64,4096]{1,0:T(8,128)(2,1)S(1)} collective-permute-done((bf16[64,4096]{1,0:T(8,128)(2,1)}, bf16[64,4096]{1,0:T(8,128)(2,1)S(1)}, u32[]{:S(2)}, u32[]{:S(2)}) %collective-permute-start) | collective-permute-done | bytes 524320 | tf_op jit(solution)/shard_map/ppermute | solution.py:336
  20.3 9.2 %collective-permute-done.2.refs_2_ = bf16[64,4224]{1,0:T(8,128)(2,1)S(1)} collective-permute-done((bf16[64,4224]{1,0:T(8,128)(2,1)S(1)}, bf16[64,4224]{1,0:T(8,128)(2,1)S(1)}, u32[]{:S(2)}, u32[]{:S(2)}) %collective-permute-start.2) | collective-permute-done | bytes 540704 | tf_op jit(solution)/shard_map/ppermute | solution.py:33
  44.7 3.5 %pack.1 = (bf16[128,32,128]{2,1,0:T(8,128)(2,1)S(1)}, bf16[192,32,128]{2,1,0:T(8,128)(2,1)S(1)}, bf16[192,32,128]{2,1,0:T(8,128)(2,1)S(1)}, bf16[128,32,128]{2,1...) custom-call(s32[2,4,8,16]{3,2,1,0:T(8,128)S(1)} %pad_add_fusion.asked_ref, ...), custom_call_target="tpu_custom_call" | custom-call | tf_op jit(solution)/shard_map/pack/pallas_call | solution.py:61
  53.6 28.6 %collective-permute-done.12.refs_1_ = bf16[192,32,128]{2,1,0:T(8,128)(2,1)S(1)} collective-permute-done((bf16[192,32,128]{2,1,0:T(8,128)(2,1)S(1)}, bf16[192,32,128]{2,1,0:T(8,128)(2,1)S(1)}, u32[]{:S(2)}, u32[]{:S(2)}) %collective-permute-start.12) | collective-permute-done | bytes 1572896 | tf_op jit(solution)/shard_map/ppermute | solution.py:33
  83.9 3.2 %collective-permute-start.15 = (bf16[64,32,128]{2,1,0:T(8,128)(2,1)}, bf16[64,32,128]{2,1,0:T(8,128)(2,1)}, u32[]{:S(2)}, u32[]{:S(2)}) collective-permute-start(bf16[64,32,128]{2,1,0:T(8,128)(2,1)} %slice.213), channel_id=1, source_target_pairs={{0,8},{4,12},{8,16},{12,20},{16,24},{20,28},{24,0},{28,4},{32,40},... | collective-permute-start | bytes 1572872 | tf_op jit(solution)/shard_map/ppermute | solution.py:33
  93.9 3.4 %collective-permute-start.24 = (bf16[64,4096]{1,0:T(8,128)(2,1)}, bf16[64,4096]{1,0:T(8,128)(2,1)}, u32[]{:S(2)}, u32[]{:S(2)}) collective-permute-start(bf16[64,4096]{1,0:T(8,128)(2,1)} %param.11), channel_id=1, source_target_pairs={{0,2},{1,3},{2,0},{3,1},{4,6},{5,7},{6,4},{7,5},{8,10},{9,11},{10,... | collective-permute-start | bytes 1572872 | tf_op jit(solution)/shard_map/ppermute | solution.py:305
  98.7 3.8 %collective-permute-done.19.refs_9_ = bf16[64,32,128]{2,1,0:T(8,128)(2,1)} collective-permute-done((bf16[64,32,128]{2,1,0:T(8,128)(2,1)}, bf16[64,32,128]{2,1,0:T(8,128)(2,1)}, u32[]{:S(2)}, u32[]{:S(2)}) %collective-permute-start.19) | collective-permute-done | bytes 524320 | tf_op jit(solution)/shard_map/ppermute | solution.py:33
  107.8 14.7 %aggregate.1 = bf16[64,4096]{1,0:T(8,128)(2,1)} custom-call(s32[32,16]{1,0:T(8,128)S(1)} %get-tuple-element.153.slot_a_ref, s32[32,16]{1,0:T(8,128)S(1)} %get-tuple-element.152.slot_b_ref, bf16[128,32,128]{2,1,0:T(8,128)(2,1)S(1)} %copy-done.5, bf16[192,32,128]{2,1,0:T(8,128)(2,1)S(1)} %collective-permute-done.12.refs_1_, ...), custom_call_target="tpu_custom_call" | custom-call | tf_op jit(solution)/shard_map/aggregate/pallas_call | solution.py:125
  122.5 3.3 %collective-permute-start.21 = (bf16[64,4096]{1,0:T(8,128)(2,1)}, bf16[64,4096]{1,0:T(8,128)(2,1)S(1)}, u32[]{:S(2)}, u32[]{:S(2)}) collective-permute-start(bf16[64,4096]{1,0:T(8,128)(2,1)} %aggregate.1), channel_id=1, source_target_pairs={{0,2},{1,3},{2,0},{3,1},{4,6},{5,7},{6,4},{7,5},{8,10},{9,11},{10,... | collective-permute-start | bytes 1572872 | tf_op jit(solution)/shard_map/ppermute | solution.py:305
  126.5 7.0 %collective-permute-done.21 = bf16[64,4096]{1,0:T(8,128)(2,1)S(1)} collective-permute-done((bf16[64,4096]{1,0:T(8,128)(2,1)}, bf16[64,4096]{1,0:T(8,128)(2,1)S(1)}, u32[]{:S(2)}, u32[]{:S(2)}) %collective-permute-start.21) | collective-permute-done | bytes 524320 | tf_op jit(solution)/shard_map/ppermute | solution.py:305
  133.6 3.3 %collective-permute-start.10 = (f32[264,64]{0,1:T(8,128)S(1)}, f32[264,64]{0,1:T(8,128)S(1)}, u32[]{:S(2)}, u32[]{:S(2)}) collective-permute-start(f32[264,64]{0,1:T(8,128)S(1)} %pad_maximum_fusion.5), channel_id=1, source_target_pairs={{0,2},{1,3},{2,0},{3,1},{4,6},{5,7},{6,4},{7,5},{8,10},{9,11},{10,... | collective-permute-start | bytes 202760 | tf_op jit(solution)/shard_map/ppermute | solution.py:305
  136.9 3.5 %collective-permute-done.10 = f32[264,64]{0,1:T(8,128)S(1)} collective-permute-done((f32[264,64]{0,1:T(8,128)S(1)}, f32[264,64]{0,1:T(8,128)S(1)}, u32[]{:S(2)}, u32[]{:S(2)}) %collective-permute-start.10) | collective-permute-done | bytes 67616 | tf_op jit(solution)/shard_map/ppermute | solution.py:305
  143.3 4.7 %multiply_convert_fusion = (bf16[256,4096]{1,0:T(8,128)(2,1)S(1)}, f32[256,4096]{1,0:T(8,128)S(1)}, f32[256,4096]{1,0:T(8,128)}) fusion(bf16[64,4096]{1,0:T(8,128)(2,1)S(1)} %collective-permute-done.25, bf16[64,4096]{1,0:T(8,128)(2,1)} %collective-permute-done.24, bf16[64,4096]{1,0:T(8,128)(2,1)S(1)} %collective-permute-done.23, ...), kind=kOutput, calls=%fused_computation.2 | convolution fusion | flops 564658176 | bytes 14812160 | tf_op jit(solution)/shard_map/dot_general | solution.py:373
  148.5 15.0 %spread.1 = (bf16[128,32,128]{2,1,0:T(8,128)(2,1)S(1)}, bf16[192,32,128]{2,1,0:T(8,128)(2,1)S(1)}, bf16[192,32,128]{2,1,0:T(8,128)(2,1)S(1)}, bf16[128,32,128]{2...) custom-call(s32[32,16]{1,0:T(8,128)S(1)} %get-tuple-element.153.slot_a_ref, ...), custom_call_target="tpu_custom_call" | custom-call | tf_op jit(solution)/shard_map/spread/pallas_call | solution.py:173
  175.3 26.2 %collective-permute-done.31 = f32[72,256]{1,0:T(8,128)S(1)} collective-permute-done((f32[72,256]{1,0:T(8,128)S(1)}, f32[72,256]{1,0:T(8,128)S(1)}, u32[]{:S(2)}, u32[]{:S(2)}) %collective-permute-start.31) | collective-permute-done | bytes 73760 | tf_op jit(solution)/shard_map/ppermute | solution.py:320
  210.2 11.5 %collective-permute-done.36 = f32[72,256]{1,0:T(8,128)S(1)} collective-permute-done((f32[72,256]{1,0:T(8,128)S(1)}, f32[72,256]{1,0:T(8,128)S(1)}, u32[]{:S(2)}, u32[]{:S(2)}) %collective-permute-start.36) | collective-permute-done | bytes 73760 | tf_op jit(solution)/shard_map/ppermute | solution.py:320
  221.7 8.3 %fold.1 = (f32[32,4096]{1,0:T(8,128)S(1)}, bf16[48,4096]{1,0:T(8,128)(2,1)S(1)}, bf16[48,4096]{1,0:T(8,128)(2,1)S(1)}, f32[32,4096]{1,0:T(8,128)S(1)}, bf16[48,4...) custom-call(s32[2,4,8,16]{3,2,1,0:T(8,128)S(1)} %pad_add_fusion.aske, ...), custom_call_target="tpu_custom_call" | custom-call | tf_op jit(solution)/shard_map/fold/pallas_call | solution.py:245
  230.2 3.2 %collective-permute-start.38 = (bf16[48,4096]{1,0:T(8,128)(2,1)S(1)}, bf16[48,4096]{1,0:T(8,128)(2,1)S(1)}, u32[]{:S(2)}, u32[]{:S(2)}) collective-permute-start(bf16[48,4096]{1,0:T(8,128)(2,1)S(1)} %get-tuple-element.112), channel_id=1, source_target_pairs={{0,96},{4,100},{8,104},{12,108},{16,112},{20,116},{24,120},{28,124... | collective-permute-start | bytes 1179656 | tf_op jit(solution)/shard_map/ppermute | solution.py:33
  236.3 4.3 %collective-permute-done.41 = f32[72,256]{1,0:T(8,128)S(1)} collective-permute-done((f32[72,256]{1,0:T(8,128)S(1)}, f32[72,256]{1,0:T(8,128)S(1)}, u32[]{:S(2)}, u32[]{:S(2)}) %collective-permute-start.41) | collective-permute-done | bytes 73760 | tf_op jit(solution)/shard_map/ppermute | solution.py:320
  241.6 5.1 %collective-permute-done.40 = bf16[48,4096]{1,0:T(8,128)(2,1)S(1)} collective-permute-done((bf16[48,4096]{1,0:T(8,128)(2,1)S(1)}, bf16[48,4096]{1,0:T(8,128)(2,1)S(1)}, u32[]{:S(2)}, u32[]{:S(2)}) %collective-permute-start.40) | collective-permute-done | bytes 393248 | tf_op jit(solution)/shard_map/ppermute | solution.py:33
  246.8 3.2 %collective-permute-start.44 = (bf16[16,4096]{1,0:T(8,128)(2,1)S(1)}, bf16[16,4096]{1,0:T(8,128)(2,1)S(1)}, u32[]{:S(2)}, u32[]{:S(2)}) collective-permute-start(bf16[16,4096]{1,0:T(8,128)(2,1)S(1)} %slice.185), channel_id=1, source_target_pairs={{0,8},{4,12},{8,16},{12,20},{16,24},{20,28},{24,0},{28,4},{32,40},... | collective-permute-start | bytes 393224 | tf_op jit(solution)/shard_map/ppermute | solution.py:33
  253.3 3.5 %collective-permute-done.46 = f32[72,256]{1,0:T(8,128)S(1)} collective-permute-done((f32[72,256]{1,0:T(8,128)S(1)}, f32[72,256]{1,0:T(8,128)S(1)}, u32[]{:S(2)}, u32[]{:S(2)}) %collective-permute-start.46) | collective-permute-done | bytes 73760 | tf_op jit(solution)/shard_map/ppermute | solution.py:320
  259.4 3.2 %collective-permute-start.48 = (bf16[48,4096]{1,0:T(8,128)(2,1)S(1)}, bf16[48,4096]{1,0:T(8,128)(2,1)S(1)}, u32[]{:S(2)}, u32[]{:S(2)}) collective-permute-start(bf16[48,4096]{1,0:T(8,128)(2,1)S(1)} %get-tuple-element.130), channel_id=1, source_target_pairs={{0,96},{4,100},{8,104},{12,108},{16,112},{20,116},{24,120},{28,124... | collective-permute-start | bytes 1179656 | tf_op jit(solution)/shard_map/ppermute | solution.py:33
  268.6 3.3 %collective-permute-start.50 = (bf16[16,4096]{1,0:T(8,128)(2,1)S(1)}, bf16[16,4096]{1,0:T(8,128)(2,1)S(1)}, u32[]{:S(2)}, u32[]{:S(2)}) collective-permute-start(bf16[16,4096]{1,0:T(8,128)(2,1)S(1)} %slice.222), channel_id=1, source_target_pairs={{0,96},{4,100},{8,104},{12,108},{16,112},{20,116},{24,120},{28,124... | collective-permute-start | bytes 393224 | tf_op jit(solution)/shard_map/ppermute | solution.py:33
  (211 shorter events, 98.0 us)
Async XLA Ops:
  0.6 14.1 %collective-permute-start = (bf16[64,4096]{1,0:T(8,128)(2,1)}, bf16[64,4096]{1,0:T(8,128)(2,1)S(1)}, u32[]{:S(2)}, u32[]{:S(2)}) collective-permute-start(bf16[64,4096]{1,0:T(8,128)(2,1)} %param.6), channel_id=1, source_target_pairs={{0,4},{4,0},{8,12},{12,8},{16,20},{20,16},{24,28},{28,24},{32,36},... | collective-permute-start | bytes 1572872 | tf_op jit(solution)/shard_map/ppermute | solution.py:336
  14.9 14.6 %collective-permute-start.2 = (bf16[64,4224]{1,0:T(8,128)(2,1)S(1)}, bf16[64,4224]{1,0:T(8,128)(2,1)S(1)}, u32[]{:S(2)}, u32[]{:S(2)}) collective-permute-start(bf16[64,4224]{1,0:T(8,128)(2,1)S(1)} %fusion.4.refs_0_), channel_id=1, source_target_pairs={{0,32},{4,36},{8,40},{12,44},{16,48},{20,52},{24,56},{28,60},{32,6... | collective-permute-start | bytes 1622024 | tf_op jit(solution)/shard_map/ppermute | solution.py:33
  16.4 14.1 %collective-permute-start.1 = (bf16[64,4224]{1,0:T(8,128)(2,1)S(1)}, bf16[64,4224]{1,0:T(8,128)(2,1)S(1)}, u32[]{:S(2)}, u32[]{:S(2)}) collective-permute-start(bf16[64,4224]{1,0:T(8,128)(2,1)S(1)} %fusion.4.refs_0_), channel_id=1, source_target_pairs={{0,96},{4,100},{8,104},{12,108},{16,112},{20,116},{24,120},{28,124... | collective-permute-start | bytes 1622024 | tf_op jit(solution)/shard_map/ppermute | solution.py:33
  18.2 16.0 %collective-permute-start.6 = (bf16[64,4224]{1,0:T(8,128)(2,1)S(1)}, bf16[64,4224]{1,0:T(8,128)(2,1)S(1)}, u32[]{:S(2)}, u32[]{:S(2)}) collective-permute-start(bf16[64,4224]{1,0:T(8,128)(2,1)S(1)} %fusion.5.refs_5_), channel_id=1, source_target_pairs={{0,8},{4,12},{8,16},{12,20},{16,24},{20,28},{24,0},{28,4},{32,40},... | collective-permute-start | bytes 1622024 | tf_op jit(solution)/shard_map/ppermute | solution.py:33
  18.5 16.7 %collective-permute-start.5 = (bf16[64,4224]{1,0:T(8,128)(2,1)S(1)}, bf16[64,4224]{1,0:T(8,128)(2,1)S(1)}, u32[]{:S(2)}, u32[]{:S(2)}) collective-permute-start(bf16[64,4224]{1,0:T(8,128)(2,1)S(1)} %fusion.5.refs_5_), channel_id=1, source_target_pairs={{0,24},{4,28},{8,0},{12,4},{16,8},{20,12},{24,16},{28,20},{32,56},... | collective-permute-start | bytes 1622024 | tf_op jit(solution)/shard_map/ppermute | solution.py:33
  48.3 33.9 %collective-permute-start.12 = (bf16[192,32,128]{2,1,0:T(8,128)(2,1)S(1)}, bf16[192,32,128]{2,1,0:T(8,128)(2,1)S(1)}, u32[]{:S(2)}, u32[]{:S(2)}) collective-permute-start(bf16[192,32,128]{2,1,0:T(8,128)(2,1)S(1)} %get-tuple-element.83), channel_id=1, source_target_pairs={{0,24},{4,28},{8,0},{12,4},{16,8},{20,12},{24,16},{28,20},{32,56},... | collective-permute-start | bytes 4718600 | tf_op jit(solution)/shard_map/ppermute | solution.py:33
  48.9 34.2 %collective-permute-start.13 = (bf16[192,32,128]{2,1,0:T(8,128)(2,1)S(1)}, bf16[192,32,128]{2,1,0:T(8,128)(2,1)S(1)}, u32[]{:S(2)}, u32[]{:S(2)}) collective-permute-start(bf16[192,32,128]{2,1,0:T(8,128)(2,1)S(1)} %get-tuple-element.84), channel_id=1, source_target_pairs={{0,8},{4,12},{8,16},{12,20},{16,24},{20,28},{24,0},{28,4},{32,40},... | collective-permute-start | bytes 4718600 | tf_op jit(solution)/shard_map/ppermute | solution.py:33
  51.6 35.5 %collective-permute-start.16 = (bf16[192,32,128]{2,1,0:T(8,128)(2,1)S(1)}, bf16[192,32,128]{2,1,0:T(8,128)(2,1)S(1)}, u32[]{:S(2)}, u32[]{:S(2)}) collective-permute-start(bf16[192,32,128]{2,1,0:T(8,128)(2,1)S(1)} %get-tuple-element.86), channel_id=1, source_target_pairs={{0,96},{4,100},{8,104},{12,108},{16,112},{20,116},{24,120},{28,124... | collective-permute-start | bytes 4718600 | tf_op jit(solution)/shard_map/ppermute | solution.py:33
  51.9 37.9 %collective-permute-start.17 = (bf16[192,32,128]{2,1,0:T(8,128)(2,1)S(1)}, bf16[192,32,128]{2,1,0:T(8,128)(2,1)S(1)}, u32[]{:S(2)}, u32[]{:S(2)}) collective-permute-start(bf16[192,32,128]{2,1,0:T(8,128)(2,1)S(1)} %get-tuple-element.87), channel_id=1, source_target_pairs={{0,32},{4,36},{8,40},{12,44},{16,48},{20,52},{24,56},{28,60},{32,6... | collective-permute-start | bytes 4718600 | tf_op jit(solution)/shard_map/ppermute | solution.py:33
  83.1 14.3 %collective-permute-start.14 = (bf16[64,32,128]{2,1,0:T(8,128)(2,1)}, bf16[64,32,128]{2,1,0:T(8,128)(2,1)}, u32[]{:S(2)}, u32[]{:S(2)}) collective-permute-start(bf16[64,32,128]{2,1,0:T(8,128)(2,1)} %slice.212), channel_id=1, source_target_pairs={{0,24},{4,28},{8,0},{12,4},{16,8},{20,12},{24,16},{28,20},{32,56},... | collective-permute-start | bytes 1572872 | tf_op jit(solution)/shard_map/ppermute | solution.py:33
  83.9 13.5 %collective-permute-start.15 = (bf16[64,32,128]{2,1,0:T(8,128)(2,1)}, bf16[64,32,128]{2,1,0:T(8,128)(2,1)}, u32[]{:S(2)}, u32[]{:S(2)}) collective-permute-start(bf16[64,32,128]{2,1,0:T(8,128)(2,1)} %slice.213), channel_id=1, source_target_pairs={{0,8},{4,12},{8,16},{12,20},{16,24},{20,28},{24,0},{28,4},{32,40},... | collective-permute-start | bytes 1572872 | tf_op jit(solution)/shard_map/ppermute | solution.py:33
  93.9 31.9 %collective-permute-start.24 = (bf16[64,4096]{1,0:T(8,128)(2,1)}, bf16[64,4096]{1,0:T(8,128)(2,1)}, u32[]{:S(2)}, u32[]{:S(2)}) collective-permute-start(bf16[64,4096]{1,0:T(8,128)(2,1)} %param.11), channel_id=1, source_target_pairs={{0,2},{1,3},{2,0},{3,1},{4,6},{5,7},{6,4},{7,5},{8,10},{9,11},{10,... | collective-permute-start | bytes 1572872 | tf_op jit(solution)/shard_map/ppermute | solution.py:305
  125.8 17.5 %collective-permute-start.23 = (bf16[64,4096]{1,0:T(8,128)(2,1)}, bf16[64,4096]{1,0:T(8,128)(2,1)S(1)}, u32[]{:S(2)}, u32[]{:S(2)}) collective-permute-start(bf16[64,4096]{1,0:T(8,128)(2,1)} %param.11), channel_id=1, source_target_pairs={{0,1},{1,0},{2,3},{3,2},{4,5},{5,4},{6,7},{7,6},{8,9},{9,8},{10,11... | collective-permute-start | bytes 1572872 | tf_op jit(solution)/shard_map/ppermute | solution.py:305
  125.8 17.5 %collective-permute-start.25 = (bf16[64,4096]{1,0:T(8,128)(2,1)}, bf16[64,4096]{1,0:T(8,128)(2,1)S(1)}, u32[]{:S(2)}, u32[]{:S(2)}) collective-permute-start(bf16[64,4096]{1,0:T(8,128)(2,1)} %collective-permute-done.24), channel_id=1, source_target_pairs={{0,1},{1,0},{2,3},{3,2},{4,5},{5,4},{6,7},{7,6},{8,9},{9,8},{10,11... | collective-permute-start | bytes 1572872 | tf_op jit(solution)/shard_map/ppermute | solution.py:305
  126.4 16.9 %collective-permute-start.20 = (bf16[64,4096]{1,0:T(8,128)(2,1)}, bf16[64,4096]{1,0:T(8,128)(2,1)S(1)}, u32[]{:S(2)}, u32[]{:S(2)}) collective-permute-start(bf16[64,4096]{1,0:T(8,128)(2,1)} %aggregate.1), channel_id=1, source_target_pairs={{0,1},{1,0},{2,3},{3,2},{4,5},{5,4},{6,7},{7,6},{8,9},{9,8},{10,11... | collective-permute-start | bytes 1572872 | tf_op jit(solution)/shard_map/ppermute | solution.py:305
  163.5 38.0 %collective-permute-start.26 = (bf16[192,32,128]{2,1,0:T(8,128)(2,1)S(1)}, bf16[192,32,128]{2,1,0:T(8,128)(2,1)S(1)}, u32[]{:S(2)}, u32[]{:S(2)}) collective-permute-start(bf16[192,32,128]{2,1,0:T(8,128)(2,1)S(1)} %get-tuple-element.90), channel_id=1, source_target_pairs={{0,8},{4,12},{8,16},{12,20},{16,24},{20,28},{24,0},{28,4},{32,40},... | collective-permute-start | bytes 4718600 | tf_op jit(solution)/shard_map/ppermute | solution.py:33
  163.5 38.1 %collective-permute-start.27 = (bf16[192,32,128]{2,1,0:T(8,128)(2,1)S(1)}, bf16[192,32,128]{2,1,0:T(8,128)(2,1)S(1)}, u32[]{:S(2)}, u32[]{:S(2)}) collective-permute-start(bf16[192,32,128]{2,1,0:T(8,128)(2,1)S(1)} %get-tuple-element.91), channel_id=1, source_target_pairs={{0,24},{4,28},{8,0},{12,4},{16,8},{20,12},{24,16},{28,20},{32,56},... | collective-permute-start | bytes 4718600 | tf_op jit(solution)/shard_map/ppermute | solution.py:33
  165.5 37.3 %collective-permute-start.28 = (bf16[192,32,128]{2,1,0:T(8,128)(2,1)}, bf16[192,32,128]{2,1,0:T(8,128)(2,1)S(1)}, u32[]{:S(2)}, u32[]{:S(2)}) collective-permute-start(bf16[192,32,128]{2,1,0:T(8,128)(2,1)} %get-tuple-element.92), channel_id=1, source_target_pairs={{0,32},{4,36},{8,40},{12,44},{16,48},{20,52},{24,56},{28,60},{32,6... | collective-permute-start | bytes 4718600 | tf_op jit(solution)/shard_map/ppermute | solution.py:33
  165.7 37.1 %collective-permute-start.29 = (bf16[192,32,128]{2,1,0:T(8,128)(2,1)}, bf16[192,32,128]{2,1,0:T(8,128)(2,1)S(1)}, u32[]{:S(2)}, u32[]{:S(2)}) collective-permute-start(bf16[192,32,128]{2,1,0:T(8,128)(2,1)} %get-tuple-element.93), channel_id=1, source_target_pairs={{0,96},{4,100},{8,104},{12,108},{16,112},{20,116},{24,120},{28,124... | collective-permute-start | bytes 4718600 | tf_op jit(solution)/shard_map/ppermute | solution.py:33
  175.2 26.3 %collective-permute-start.31 = (f32[72,256]{1,0:T(8,128)S(1)}, f32[72,256]{1,0:T(8,128)S(1)}, u32[]{:S(2)}, u32[]{:S(2)}) collective-permute-start(f32[72,256]{1,0:T(8,128)S(1)} %fusion.39), channel_id=1, source_target_pairs={{0,8},{4,12},{8,0},{12,4},{16,24},{20,28},{24,16},{28,20},{32,40},... | collective-permute-start | bytes 221192 | tf_op jit(solution)/shard_map/ppermute | solution.py:320
  204.0 17.7 %collective-permute-start.35 = (bf16[64,32,128]{2,1,0:T(8,128)(2,1)S(1)}, bf16[64,32,128]{2,1,0:T(8,128)(2,1)S(1)}, u32[]{:S(2)}, u32[]{:S(2)}) collective-permute-start(bf16[64,32,128]{2,1,0:T(8,128)(2,1)S(1)} %slice.178), channel_id=1, source_target_pairs={{0,96},{4,100},{8,104},{12,108},{16,112},{20,116},{24,120},{28,124... | collective-permute-start | bytes 1572872 | tf_op jit(solution)/shard_map/ppermute | solution.py:33
  206.9 14.8 %collective-permute-start.34 = (bf16[64,32,128]{2,1,0:T(8,128)(2,1)S(1)}, bf16[64,32,128]{2,1,0:T(8,128)(2,1)S(1)}, u32[]{:S(2)}, u32[]{:S(2)}) collective-permute-start(bf16[64,32,128]{2,1,0:T(8,128)(2,1)S(1)} %slice.177), channel_id=1, source_target_pairs={{0,32},{4,36},{8,40},{12,44},{16,48},{20,52},{24,56},{28,60},{32,6... | collective-permute-start | bytes 1572872 | tf_op jit(solution)/shard_map/ppermute | solution.py:33
  206.9 14.8 %collective-permute-start.33 = (bf16[64,32,128]{2,1,0:T(8,128)(2,1)S(1)}, bf16[64,32,128]{2,1,0:T(8,128)(2,1)S(1)}, u32[]{:S(2)}, u32[]{:S(2)}) collective-permute-start(bf16[64,32,128]{2,1,0:T(8,128)(2,1)S(1)} %slice.176), channel_id=1, source_target_pairs={{0,24},{4,28},{8,0},{12,4},{16,8},{20,12},{24,16},{28,20},{32,56},... | collective-permute-start | bytes 1572872 | tf_op jit(solution)/shard_map/ppermute | solution.py:33
  207.2 14.5 %collective-permute-start.32 = (bf16[64,32,128]{2,1,0:T(8,128)(2,1)S(1)}, bf16[64,32,128]{2,1,0:T(8,128)(2,1)S(1)}, u32[]{:S(2)}, u32[]{:S(2)}) collective-permute-start(bf16[64,32,128]{2,1,0:T(8,128)(2,1)S(1)} %slice.175), channel_id=1, source_target_pairs={{0,8},{4,12},{8,16},{12,20},{16,24},{20,28},{24,0},{28,4},{32,40},... | collective-permute-start | bytes 1572872 | tf_op jit(solution)/shard_map/ppermute | solution.py:33
  (47 other events, 488.0 us)
where the time goes:
time: 284 us; the launch traced here: 282 us
  waiting for transfers between devices  133 us (47%)
  starting transfers between devices  71.9 us (25%)
  Pallas kernels  41.5 us (15%)
  local copies, waits for them, and re-layouts  19.4 us (7%)
  other arithmetic  8.17 us (3%)
  matrix products  6.97 us (2%)
    ppermute x40, waiting for transfers between devices, shift(): lax.ppermute(v, 'rows', row_perm(near, far, 0) if near_axis == 0 else row...  63.4 us
    ppermute x40, starting transfers between devices, shift(): lax.ppermute(v, 'rows', row_perm(near, far, 0) if near_axis == 0 else row...  55.1 us
    ppermute x5, waiting for transfers between devices, row_swap(): return v + lax.ppermute(v, 'rows', pairs)  48.6 us
    pallas_call x1, Pallas kernels, spread(): pl.pallas_call(spread_kernel, out_shape=[jax.ShapeDtypeStruct((n, half, T...  15 us
    pallas_call x1, Pallas kernels, aggregate(): pl.pallas_call(aggregate_kernel, out_shape=jax.ShapeDtypeStruct((2 * half...  14.7 us
    ppermute x9, waiting for transfers between devices, from_feat(): return lax.ppermute(v, 'feat', [(i, i ^ step) for i in range(4)])  12.9 us
    ppermute x9, starting transfers between devices, from_feat(): return lax.ppermute(v, 'feat', [(i, i ^ step) for i in range(4)])  10.9 us
    unnamed x31, local copies, waits for them, and re-layouts  10 us
  transfers between devices with their start and end apart: 56, of which 26 were waited for; matrix products, arithmetic and copies ran while one was open for 6% of the time, Pallas kernels for 5%

commit v1 on v0

--- a/solution.py
+++ b/solution.py
@@ -31,6 +31,10 @@
 
 def shift(v, near_axis, near, far):
     return lax.ppermute(v, "rows", row_perm(near, far, 0) if near_axis == 0 else row_perm(far, near, 0))
+
+
+def in_hbm(*arrays):
+    return [pltpu.with_memory_space_constraint(v, pltpu.HBM) for v in arrays]
 
 
 def pack_kernel(asked_ref, *refs):
@@ -65,7 +69,7 @@
         ],
         in_specs=[pl.BlockSpec(memory_space=pltpu.SMEM)] + [vmem] * len(sources),
         out_specs=[vmem] * 6,
-        compiler_params=pltpu.CompilerParams(vmem_limit_bytes=40 * MIB),
+        compiler_params=pltpu.CompilerParams(vmem_limit_bytes=18 * MIB),
         name="pack",
     )(asked, *sources)
     return out[:3], out[3:]
@@ -113,9 +117,9 @@
         b = jnp.concatenate([b_ref[slot_b_ref[i, s]] for s in range(slots)], axis=1)
         tiles = jnp.concatenate([vals_ref[j, s] for s in range(slots)], axis=1)
         out = lax.dot_general(
-            jnp.concatenate([a, b], axis=0), tiles, (((1,), (1,)), ((), ())), preferred_element_type=jnp.float32
+            tiles, jnp.concatenate([a, b], axis=0), (((1,), (1,)), ((), ())), preferred_element_type=jnp.float32
         )
-        out_ref[:, j * TB : (j + 1) * TB] = out.astype(out_ref.dtype)
+        out_ref[:, j * TB : (j + 1) * TB] = out.T.astype(out_ref.dtype)
 
 
 def aggregate(slot_a, slot_b, got_a, got_b, vals):
@@ -134,9 +138,9 @@
             scratch_shapes=[pltpu.VMEM((SIDE * PART, half, TB), jnp.bfloat16)] * 2
             + [pltpu.SemaphoreType.DMA((2 * len(LAID),))],
         ),
-        compiler_params=pltpu.CompilerParams(vmem_limit_bytes=40 * MIB),
+        compiler_params=pltpu.CompilerParams(vmem_limit_bytes=16 * MIB),
         name="aggregate",
-    )(slot_a, slot_b, *got_a, *got_b, vals)
+    )(slot_a, slot_b, *in_hbm(*got_a, *got_b, vals))
 
 
 def spread_kernel(slot_a_ref, slot_b_ref, mix_ref, vals_ref, *refs):
@@ -153,8 +157,10 @@
     for j in range(per):
         i = step * per + j
         mix = mix_ref[:, j * TB : (j + 1) * TB]
+        tiles = jnp.concatenate([vals_ref[j, s] for s in range(slots)], axis=1)
+        terms = jnp.dot(mix, tiles, preferred_element_type=jnp.float32)
         for s in range(slots):
-            term = jnp.dot(mix, vals_ref[j, s], preferred_element_type=jnp.float32)
+            term = terms[:, s * TB : (s + 1) * TB]
             a_ref[slot_a_ref[i, s]] += term[:half]
             b_ref[slot_b_ref[i, s]] += term[half:]
 
@@ -186,9 +192,9 @@
             ],
             scratch_shapes=[pltpu.VMEM((SIDE * PART, half, TB), jnp.float32)] * 2,
         ),
-        compiler_params=pltpu.CompilerParams(vmem_limit_bytes=48 * MIB),
+        compiler_params=pltpu.CompilerParams(vmem_limit_bytes=34 * MIB),
         name="spread",
-    )(slot_a, slot_b, mix, vals)
+    )(slot_a, slot_b, mix, *in_hbm(vals))
     return out[:3], out[3:]
 
 
@@ -214,25 +220,12 @@
         pl.when(p < NEAR // 2)(functools.partial(add, upper, 2))
         pl.when(p >= NEAR // 2)(functools.partial(add, lower, 2))
         for plane in range(PLANES):
-            own, plus, minus = outs[(h * PLANES + plane) * 3 :][:3]
-            half = own.shape[0]
-
-            @pl.when(p == plane)
-            def _():
-                own[...] = acc_ref[...]
-
-            @pl.when(p == PLANES + plane)
-            def _():
-                plus[:half] = acc_ref[...].astype(plus.dtype)
-
-            @pl.when(p == 2 * PLANES + plane)
-            def _():
-                plus[half:] = acc_ref[: half // 2].astype(plus.dtype)
-                minus[half:] = acc_ref[half // 2 :].astype(minus.dtype)
-
-            @pl.when(p == 3 * PLANES + plane)
-            def _():
-                minus[:half] = acc_ref[...].astype(minus.dtype)
+            for near in range(SIDE):
+
+                @pl.when(p == near * PLANES + plane)
+                def _():
+                    out = outs[(h * PLANES + plane) * SIDE + near]
+                    out[...] = acc_ref[...].astype(out.dtype)
 
 
 def fold(asked, got, width):
@@ -244,42 +237,31 @@
     ]
     out = pl.pallas_call(
         fold_kernel,
-        out_shape=[
-            jax.ShapeDtypeStruct((half, width), jnp.float32),
-            jax.ShapeDtypeStruct((half * 3 // 2, width), jnp.bfloat16),
-            jax.ShapeDtypeStruct((half * 3 // 2, width), jnp.bfloat16),
-        ]
+        out_shape=([jax.ShapeDtypeStruct((half, width), jnp.float32)]
+            + [jax.ShapeDtypeStruct((half, width), jnp.bfloat16)] * (SIDE - 1))
         * (2 * PLANES),
         grid_spec=pltpu.PrefetchScalarGridSpec(
             num_scalar_prefetch=1,
             grid=(NEAR,),
             in_specs=specs * 2,
-            out_specs=[
-                pl.BlockSpec((rows, width), lambda p, a: (0, 0), pipeline_mode=pl.Buffered(1))
-                for rows in (half, half * 3 // 2, half * 3 // 2) * (2 * PLANES)
-            ],
+            out_specs=[pl.BlockSpec((half, width), lambda p, a: (0, 0), pipeline_mode=pl.Buffered(1))] * (2 * NEAR),
             scratch_shapes=[pltpu.VMEM((half, width), jnp.float32)],
         ),
-        compiler_params=pltpu.CompilerParams(vmem_limit_bytes=40 * MIB),
+        compiler_params=pltpu.CompilerParams(vmem_limit_bytes=14 * MIB),
         name="fold",
     )(asked, *got)
-    return [[out[(h * PLANES + plane) * 3 :][:3] for plane in range(PLANES)] for h in range(2)]
-
-
-def line_sum(folded, plane, side=None):
-    first = [
-        [shift(parts[plane][1], h, 1, 0), shift(parts[plane][2], h, -1, 0)] for h, parts in enumerate(folded)
-    ]
-    if side is not None:
-        first, side = lax.optimization_barrier((first, side))
+    return [[out[(h * PLANES + plane) * SIDE :][:SIDE] for plane in range(PLANES)] for h in range(2)]
+
+
+def line_sum(folded, plane):
+    came = {(h, near): shift(folded[h][plane][near], h, near, 0) for near in (2, 1, 3) for h in range(2)}
     sums = []
-    for h, (plus, minus) in enumerate(first):
-        own = folded[h][plane][0]
-        half = own.shape[0]
-        passed = [shift(plus[half:], h, 1, 0), shift(minus[half:], h, -1, 0)]
-        total = own + plus[:half].astype(jnp.float32) + minus[:half].astype(jnp.float32)
-        sums.append(total + jnp.concatenate(passed, axis=0).astype(jnp.float32))
-    return jnp.concatenate(sums, axis=0), side
+    for h in range(2):
+        total = folded[h][plane][0]
+        for near in range(1, SIDE):
+            total = total + came[h, near].astype(jnp.float32)
+        sums.append(total)
+    return jnp.concatenate(sums, axis=0)
 
 
 def requests(cols, owners, blocks):
@@ -379,24 +361,22 @@
     back_mix = jnp.dot(weight_all[:feat_loc], grad_pre, preferred_element_type=jnp.float32).astype(jnp.bfloat16)
 
     terms = spread(*slots, back_mix, tile_vals)
-
     own_grad = grad_pre[:feat_loc]
     weight_part = lax.dot_general(own_grad, agg_all, (((1,), (1,)), ((), ())), preferred_element_type=jnp.float32)
     bias_part = jnp.sum(own_grad.astype(jnp.float32), axis=1)
     bias_rows = jnp.broadcast_to(jnp.pad(bias_part, (0, weight.shape[0] - feat_loc))[None], (8, weight.shape[0]))
     parts = jnp.concatenate([weight_part, bias_rows], axis=0)
-    for step in ((0, 0, 1), (0, 1, 0)):
-        parts = row_swap(parts, *step)
+    parts = row_swap(row_swap(parts, 0, 0, 1), 0, 1, 0)
 
     back, parts = exchange(terms, 1, parts)
     parts = row_swap(parts, 0, 2, 0)
     back, parts = lax.optimization_barrier((back, parts))
     folded = fold(asked, back[0] + back[1], width)
-    passed, parts = line_sum(folded, 1, row_swap(parts, 1, 0, 0))
-    passed, parts = passed.astype(jnp.bfloat16), row_swap(parts, 2, 0, 0)
+    passed, parts = line_sum(folded, 1).astype(jnp.bfloat16), row_swap(parts, 1, 0, 0)
     passed, folded, parts = lax.optimization_barrier((passed, folded, parts))
     arrived = lax.ppermute(passed, "rows", row_perm(0, 0, 1))
-    grad_feats = line_sum(folded, 0)[0] + arrived.astype(jnp.float32)
+    grad_feats = line_sum(folded, 0) + arrived.astype(jnp.float32)
+    parts = row_swap(parts, 2, 0, 0)
     grad_bias = parts[feat_loc, :feat_loc]
     grad_weight = blocks_by_feat(parts[:feat_loc].T, mine)
     return (activated, grad_feats, grad_weight, grad_bias)

time: 284 us -> 273 us (0.961)
  waiting for transfers between devices: 133 us -> 141 us
  local copies, waits for them, and re-layouts: 19.4 us -> 11.6 us
  starting transfers between devices: 71.9 us -> 68.2 us
  Pallas kernels: 41.5 us -> 38.2 us
    ppermute x1, waiting for transfers between devices: 0.18 us -> 8.83 us  [on_device(): arrived = lax.ppermute(passed, 'rows', row_perm(0, 0, 1))]
    unnamed x31 -> x33, local copies, waits for them, and re-layouts: 10 us -> 1.89 us
    ppermute x40 -> x36, starting transfers between devices: 55.1 us -> 49.1 us  [shift(): lax.ppermute(v, 'rows', row_perm(near, far, 0) if near_axis == 0 else row...]
    ppermute x40 -> x36, waiting for transfers between devices: 63.4 us -> 65.5 us  [shift(): lax.ppermute(v, 'rows', row_perm(near, far, 0) if near_axis == 0 else row...]
  transfers between devices with their start and end apart: 56 -> 52, of which waited for: 26 -> 23; matrix products, arithmetic and copies ran while one was open for 6% -> 6% of each run, Pallas kernels for 5% -> 6%
where the time goes in v1:
time: 273 us
  waiting for transfers between devices  141 us (52%)
  starting transfers between devices  68.2 us (25%)
  Pallas kernels  38.2 us (14%)
  local copies, waits for them, and re-layouts  11.6 us (4%)
  other arithmetic  6.98 us (3%)
  matrix products  5.69 us (2%)
    ppermute x36, waiting for transfers between devices, shift(): lax.ppermute(v, 'rows', row_perm(near, far, 0) if near_axis == 0 else row...  65.5 us
    ppermute x36, starting transfers between devices, shift(): lax.ppermute(v, 'rows', row_perm(near, far, 0) if near_axis == 0 else row...  49.1 us
    ppermute x5, waiting for transfers between devices, row_swap(): return v + lax.ppermute(v, 'rows', pairs)  46.1 us
    pallas_call x1, Pallas kernels, aggregate(): pl.pallas_call(aggregate_kernel, out_shape=jax.ShapeDtypeStruct((2 * half...  15.4 us
    ppermute x9, waiting for transfers between devices, from_feat(): return lax.ppermute(v, 'feat', [(i, i ^ step) for i in range(4)])  12.7 us
    pallas_call x1, Pallas kernels, spread(): pl.pallas_call(spread_kernel, out_shape=[jax.ShapeDtypeStruct((n, half, T...  12.6 us
    ppermute x9, starting transfers between devices, from_feat(): return lax.ppermute(v, 'feat', [(i, i ^ step) for i in range(4)])  10.9 us
    ppermute x1, waiting for transfers between devices, on_device(): arrived = lax.ppermute(passed, 'rows', row_perm(0, 0, 1))  8.83 us
  transfers between devices with their start and end apart: 52, of which 23 were waited for; matrix products, arithmetic and copies ran while one was open for 6% of the time, Pallas kernels for 6%

profile of v1, /device:TPU:24, one launch (start us, length us, event | category | flops | bytes accessed | tf_op | source)
XLA Modules:
  0.0 272.9 jit_solution(11934650971453462006)
XLA Ops:
  6.8 7.9 %collective-permute-done = bf16[64,4096]{1,0:T(8,128)(2,1)S(1)} collective-permute-done((bf16[64,4096]{1,0:T(8,128)(2,1)}, bf16[64,4096]{1,0:T(8,128)(2,1)S(1)}, u32[]{:S(2)}, u32[]{:S(2)}) %collective-permute-start) | collective-permute-done | bytes 524320 | tf_op jit(solution)/shard_map/ppermute | solution.py:318
  20.3 9.2 %collective-permute-done.2.refs_2_ = bf16[64,4224]{1,0:T(8,128)(2,1)S(1)} collective-permute-done((bf16[64,4224]{1,0:T(8,128)(2,1)S(1)}, bf16[64,4224]{1,0:T(8,128)(2,1)S(1)}, u32[]{:S(2)}, u32[]{:S(2)}) %collective-permute-start.2) | collective-permute-done | bytes 540704 | tf_op jit(solution)/shard_map/ppermute | solution.py:33
  44.8 3.5 %pack.1 = (bf16[128,32,128]{2,1,0:T(8,128)(2,1)S(1)}, bf16[192,32,128]{2,1,0:T(8,128)(2,1)S(1)}, bf16[192,32,128]{2,1,0:T(8,128)(2,1)S(1)}, bf16[128,32,128]{2,1...) custom-call(s32[2,4,8,16]{3,2,1,0:T(8,128)S(1)} %pad_add_fusion.asked_ref, ...), custom_call_target="tpu_custom_call" | custom-call | tf_op jit(solution)/shard_map/pack/pallas_call | solution.py:65
  53.7 28.6 %collective-permute-done.12.refs_1_ = bf16[192,32,128]{2,1,0:T(8,128)(2,1)S(1)} collective-permute-done((bf16[192,32,128]{2,1,0:T(8,128)(2,1)S(1)}, bf16[192,32,128]{2,1,0:T(8,128)(2,1)S(1)}, u32[]{:S(2)}, u32[]{:S(2)}) %collective-permute-start.12) | collective-permute-done | bytes 1572896 | tf_op jit(solution)/shard_map/ppermute | solution.py:33
  84.1 3.2 %collective-permute-start.15 = (bf16[64,32,128]{2,1,0:T(8,128)(2,1)}, bf16[64,32,128]{2,1,0:T(8,128)(2,1)S(1)}, u32[]{:S(2)}, u32[]{:S(2)}) collective-permute-start(bf16[64,32,128]{2,1,0:T(8,128)(2,1)} %slice.149), channel_id=1, source_target_pairs={{0,8},{4,12},{8,16},{12,20},{16,24},{20,28},{24,0},{28,4},{32,40},... | collective-permute-start | bytes 1572872 | tf_op jit(solution)/shard_map/ppermute | solution.py:33
  92.4 3.4 %collective-permute-start.24 = (bf16[64,4096]{1,0:T(8,128)(2,1)S(1)}, bf16[64,4096]{1,0:T(8,128)(2,1)S(1)}, u32[]{:S(2)}, u32[]{:S(2)}) collective-permute-start(bf16[64,4096]{1,0:T(8,128)(2,1)S(1)} %copy-done.15), channel_id=1, source_target_pairs={{0,2},{1,3},{2,0},{3,1},{4,6},{5,7},{6,4},{7,5},{8,10},{9,11},{10,... | collective-permute-start | bytes 1572872 | tf_op jit(solution)/shard_map/ppermute | solution.py:287
  97.7 3.3 %collective-permute-done.19.refs_9_ = bf16[64,32,128]{2,1,0:T(8,128)(2,1)} collective-permute-done((bf16[64,32,128]{2,1,0:T(8,128)(2,1)}, bf16[64,32,128]{2,1,0:T(8,128)(2,1)}, u32[]{:S(2)}, u32[]{:S(2)}) %collective-permute-start.19) | collective-permute-done | bytes 524320 | tf_op jit(solution)/shard_map/ppermute | solution.py:33
  101.0 15.4 %aggregate.1 = bf16[64,4096]{1,0:T(8,128)(2,1)S(1)} custom-call(s32[32,16]{1,0:T(8,128)S(1)} %get-tuple-element.155.slot_a_ref, s32[32,16]{1,0:T(8,128)S(1)} %get-tuple-element.154.slot_b_ref, bf16[128,32,128]{2,1,0:T(8,128)(2,1)} %copy-done, bf16[192,32,128]{2,1,0:T(8,128)(2,1)} %copy-done.2, bf16[192,32,128]{2,1,0:T(8,128)(2,1)} %copy-done.3, ...), custom_call_target="tpu_custom_call" | custom-call | tf_op jit(solution)/shard_map/aggregate/pallas_call | solution.py:129
  116.4 3.3 %collective-permute-start.21 = (bf16[64,4096]{1,0:T(8,128)(2,1)S(1)}, bf16[64,4096]{1,0:T(8,128)(2,1)S(1)}, u32[]{:S(2)}, u32[]{:S(2)}) collective-permute-start(bf16[64,4096]{1,0:T(8,128)(2,1)S(1)} %aggregate.1), channel_id=1, source_target_pairs={{0,2},{1,3},{2,0},{3,1},{4,6},{5,7},{6,4},{7,5},{8,10},{9,11},{10,... | collective-permute-start | bytes 1572872 | tf_op jit(solution)/shard_map/ppermute | solution.py:287
  120.4 6.8 %collective-permute-done.21 = bf16[64,4096]{1,0:T(8,128)(2,1)S(1)} collective-permute-done((bf16[64,4096]{1,0:T(8,128)(2,1)S(1)}, bf16[64,4096]{1,0:T(8,128)(2,1)S(1)}, u32[]{:S(2)}, u32[]{:S(2)}) %collective-permute-start.21) | collective-permute-done | bytes 524320 | tf_op jit(solution)/shard_map/ppermute | solution.py:287
  127.2 3.3 %collective-permute-start.10 = (f32[264,64]{0,1:T(8,128)S(1)}, f32[264,64]{0,1:T(8,128)S(1)}, u32[]{:S(2)}, u32[]{:S(2)}) collective-permute-start(f32[264,64]{0,1:T(8,128)S(1)} %pad_maximum_fusion.5), channel_id=1, source_target_pairs={{0,2},{1,3},{2,0},{3,1},{4,6},{5,7},{6,4},{7,5},{8,10},{9,11},{10,... | collective-permute-start | bytes 202760 | tf_op jit(solution)/shard_map/ppermute | solution.py:287
  130.5 3.5 %collective-permute-done.10 = f32[264,64]{0,1:T(8,128)S(1)} collective-permute-done((f32[264,64]{0,1:T(8,128)S(1)}, f32[264,64]{0,1:T(8,128)S(1)}, u32[]{:S(2)}, u32[]{:S(2)}) %collective-permute-start.10) | collective-permute-done | bytes 67616 | tf_op jit(solution)/shard_map/ppermute | solution.py:287
  137.0 3.4 %multiply_convert_fusion = (bf16[256,4096]{1,0:T(8,128)(2,1)S(1)}, f32[256,4096]{1,0:T(8,128)S(1)}, f32[256,4096]{1,0:T(8,128)S(1)}) fusion(bf16[64,4096]{1,0:T(8,128)(2,1)} %collective-permute-done.25, bf16[64,4096]{1,0:T(8,128)(2,1)S(1)} %collective-permute-done.24, bf16[64,4096]{1,0:T(8,128)(2,1)} %collective-permute-done.23, ...), kind=kOutput, calls=%fused_computation.2 | convolution fusion | flops 564658176 | bytes 14812160 | tf_op jit(solution)/shard_map/dot_general | solution.py:355
  140.9 12.6 %spread.1 = (bf16[128,32,128]{2,1,0:T(8,128)(2,1)S(1)}, bf16[192,32,128]{2,1,0:T(8,128)(2,1)S(1)}, bf16[192,32,128]{2,1,0:T(8,128)(2,1)S(1)}, bf16[128,32,128]{2...) custom-call(s32[32,16]{1,0:T(8,128)S(1)} %get-tuple-element.155.slot_a_ref, ...), custom_call_target="tpu_custom_call" | custom-call | tf_op jit(solution)/shard_map/spread/pallas_call | solution.py:179
  162.2 3.1 %collective-permute-done.30 = f32[72,256]{1,0:T(8,128)S(1)} collective-permute-done((f32[72,256]{1,0:T(8,128)S(1)}, f32[72,256]{1,0:T(8,128)S(1)}, u32[]{:S(2)}, u32[]{:S(2)}) %collective-permute-start.30) | collective-permute-done | bytes 73760 | tf_op jit(solution)/shard_map/ppermute | solution.py:302
  165.4 26.2 %collective-permute-done.31 = f32[72,256]{1,0:T(8,128)S(1)} collective-permute-done((f32[72,256]{1,0:T(8,128)S(1)}, f32[72,256]{1,0:T(8,128)S(1)}, u32[]{:S(2)}, u32[]{:S(2)}) %collective-permute-start.31) | collective-permute-done | bytes 73760 | tf_op jit(solution)/shard_map/ppermute | solution.py:302
  192.9 3.0 %collective-permute-start.35 = (bf16[64,32,128]{2,1,0:T(8,128)(2,1)S(1)}, bf16[64,32,128]{2,1,0:T(8,128)(2,1)S(1)}, u32[]{:S(2)}, u32[]{:S(2)}) collective-permute-start(bf16[64,32,128]{2,1,0:T(8,128)(2,1)S(1)} %slice.130), channel_id=1, source_target_pairs={{0,96},{4,100},{8,104},{12,108},{16,112},{20,116},{24,120},{28,124... | collective-permute-start | bytes 1572872 | tf_op jit(solution)/shard_map/ppermute | solution.py:33
  199.2 11.6 %collective-permute-done.36 = f32[72,256]{1,0:T(8,128)S(1)} collective-permute-done((f32[72,256]{1,0:T(8,128)S(1)}, f32[72,256]{1,0:T(8,128)S(1)}, u32[]{:S(2)}, u32[]{:S(2)}) %collective-permute-start.36) | collective-permute-done | bytes 73760 | tf_op jit(solution)/shard_map/ppermute | solution.py:302
  210.8 6.7 %fold.1 = (f32[32,4096]{1,0:T(8,128)S(1)}, bf16[32,4096]{1,0:T(8,128)(2,1)S(1)}, bf16[32,4096]{1,0:T(8,128)(2,1)S(1)}, bf16[32,4096]{1,0:T(8,128)(2,1)S(1)}, f32...) custom-call(s32[2,4,8,16]{3,2,1,0:T(8,128)S(1)} %pad_add_fusion.aske, ...), custom_call_target="tpu_custom_call" | custom-call | tf_op jit(solution)/shard_map/fold/pallas_call | solution.py:238
  217.6 4.5 %collective-permute-start.38 = (bf16[32,4096]{1,0:T(8,128)(2,1)S(1)}, bf16[32,4096]{1,0:T(8,128)(2,1)S(1)}, u32[]{:S(2)}, u32[]{:S(2)}) collective-permute-start(bf16[32,4096]{1,0:T(8,128)(2,1)S(1)} %get-tuple-element.113), channel_id=1, source_target_pairs={{0,64},{4,68},{8,72},{12,76},{16,80},{20,84},{24,88},{28,92},{32,9... | collective-permute-start | bytes 786440 | tf_op jit(solution)/shard_map/ppermute | solution.py:33
  226.9 5.2 %collective-permute-done.43 = f32[72,256]{1,0:T(8,128)S(1)} collective-permute-done((f32[72,256]{1,0:T(8,128)S(1)}, f32[72,256]{1,0:T(8,128)S(1)}, u32[]{:S(2)}, u32[]{:S(2)}) %collective-permute-start.43) | collective-permute-done | bytes 73760 | tf_op jit(solution)/shard_map/ppermute | solution.py:302
  234.8 5.9 %collective-permute-done.41 = bf16[32,4096]{1,0:T(8,128)(2,1)S(1)} collective-permute-done((bf16[32,4096]{1,0:T(8,128)(2,1)S(1)}, bf16[32,4096]{1,0:T(8,128)(2,1)S(1)}, u32[]{:S(2)}, u32[]{:S(2)}) %collective-permute-start.41) | collective-permute-done | bytes 262176 | tf_op jit(solution)/shard_map/ppermute | solution.py:33
  255.1 4.8 %collective-permute-done.45 = bf16[32,4096]{1,0:T(8,128)(2,1)S(1)} collective-permute-done((bf16[32,4096]{1,0:T(8,128)(2,1)S(1)}, bf16[32,4096]{1,0:T(8,128)(2,1)S(1)}, u32[]{:S(2)}, u32[]{:S(2)}) %collective-permute-start.45) | collective-permute-done | bytes 262176 | tf_op jit(solution)/shard_map/ppermute | solution.py:33
  263.0 8.8 %collective-permute-done.50 = bf16[64,4096]{1,0:T(8,128)(2,1)S(1)} collective-permute-done((bf16[64,4096]{1,0:T(8,128)(2,1)S(1)}, bf16[64,4096]{1,0:T(8,128)(2,1)S(1)}, u32[]{:S(2)}, u32[]{:S(2)}) %collective-permute-start.50) | collective-permute-done | bytes 524320 | tf_op jit(solution)/shard_map/ppermute | solution.py:377
  (197 shorter events, 84.4 us)
Async XLA Ops:
  0.6 14.1 %collective-permute-start = (bf16[64,4096]{1,0:T(8,128)(2,1)}, bf16[64,4096]{1,0:T(8,128)(2,1)S(1)}, u32[]{:S(2)}, u32[]{:S(2)}) collective-permute-start(bf16[64,4096]{1,0:T(8,128)(2,1)} %param.6), channel_id=1, source_target_pairs={{0,4},{4,0},{8,12},{12,8},{16,20},{20,16},{24,28},{28,24},{32,36},... | collective-permute-start | bytes 1572872 | tf_op jit(solution)/shard_map/ppermute | solution.py:318
  14.9 14.6 %collective-permute-start.2 = (bf16[64,4224]{1,0:T(8,128)(2,1)S(1)}, bf16[64,4224]{1,0:T(8,128)(2,1)S(1)}, u32[]{:S(2)}, u32[]{:S(2)}) collective-permute-start(bf16[64,4224]{1,0:T(8,128)(2,1)S(1)} %fusion.4.refs_0_), channel_id=1, source_target_pairs={{0,32},{4,36},{8,40},{12,44},{16,48},{20,52},{24,56},{28,60},{32,6... | collective-permute-start | bytes 1622024 | tf_op jit(solution)/shard_map/ppermute | solution.py:33
  16.4 14.1 %collective-permute-start.1 = (bf16[64,4224]{1,0:T(8,128)(2,1)S(1)}, bf16[64,4224]{1,0:T(8,128)(2,1)S(1)}, u32[]{:S(2)}, u32[]{:S(2)}) collective-permute-start(bf16[64,4224]{1,0:T(8,128)(2,1)S(1)} %fusion.4.refs_0_), channel_id=1, source_target_pairs={{0,96},{4,100},{8,104},{12,108},{16,112},{20,116},{24,120},{28,124... | collective-permute-start | bytes 1622024 | tf_op jit(solution)/shard_map/ppermute | solution.py:33
  18.2 16.0 %collective-permute-start.6 = (bf16[64,4224]{1,0:T(8,128)(2,1)S(1)}, bf16[64,4224]{1,0:T(8,128)(2,1)S(1)}, u32[]{:S(2)}, u32[]{:S(2)}) collective-permute-start(bf16[64,4224]{1,0:T(8,128)(2,1)S(1)} %fusion.5.refs_5_), channel_id=1, source_target_pairs={{0,8},{4,12},{8,16},{12,20},{16,24},{20,28},{24,0},{28,4},{32,40},... | collective-permute-start | bytes 1622024 | tf_op jit(solution)/shard_map/ppermute | solution.py:33
  18.5 16.7 %collective-permute-start.5 = (bf16[64,4224]{1,0:T(8,128)(2,1)S(1)}, bf16[64,4224]{1,0:T(8,128)(2,1)S(1)}, u32[]{:S(2)}, u32[]{:S(2)}) collective-permute-start(bf16[64,4224]{1,0:T(8,128)(2,1)S(1)} %fusion.5.refs_5_), channel_id=1, source_target_pairs={{0,24},{4,28},{8,0},{12,4},{16,8},{20,12},{24,16},{28,20},{32,56},... | collective-permute-start | bytes 1622024 | tf_op jit(solution)/shard_map/ppermute | solution.py:33
  48.3 33.9 %collective-permute-start.12 = (bf16[192,32,128]{2,1,0:T(8,128)(2,1)S(1)}, bf16[192,32,128]{2,1,0:T(8,128)(2,1)S(1)}, u32[]{:S(2)}, u32[]{:S(2)}) collective-permute-start(bf16[192,32,128]{2,1,0:T(8,128)(2,1)S(1)} %get-tuple-element.84), channel_id=1, source_target_pairs={{0,24},{4,28},{8,0},{12,4},{16,8},{20,12},{24,16},{28,20},{32,56},... | collective-permute-start | bytes 4718600 | tf_op jit(solution)/shard_map/ppermute | solution.py:33
  48.9 34.3 %collective-permute-start.13 = (bf16[192,32,128]{2,1,0:T(8,128)(2,1)S(1)}, bf16[192,32,128]{2,1,0:T(8,128)(2,1)S(1)}, u32[]{:S(2)}, u32[]{:S(2)}) collective-permute-start(bf16[192,32,128]{2,1,0:T(8,128)(2,1)S(1)} %get-tuple-element.85), channel_id=1, source_target_pairs={{0,8},{4,12},{8,16},{12,20},{16,24},{20,28},{24,0},{28,4},{32,40},... | collective-permute-start | bytes 4718600 | tf_op jit(solution)/shard_map/ppermute | solution.py:33
  51.6 35.7 %collective-permute-start.16 = (bf16[192,32,128]{2,1,0:T(8,128)(2,1)S(1)}, bf16[192,32,128]{2,1,0:T(8,128)(2,1)S(1)}, u32[]{:S(2)}, u32[]{:S(2)}) collective-permute-start(bf16[192,32,128]{2,1,0:T(8,128)(2,1)S(1)} %get-tuple-element.87), channel_id=1, source_target_pairs={{0,96},{4,100},{8,104},{12,108},{16,112},{20,116},{24,120},{28,124... | collective-permute-start | bytes 4718600 | tf_op jit(solution)/shard_map/ppermute | solution.py:33
  51.9 37.0 %collective-permute-start.17 = (bf16[192,32,128]{2,1,0:T(8,128)(2,1)S(1)}, bf16[192,32,128]{2,1,0:T(8,128)(2,1)S(1)}, u32[]{:S(2)}, u32[]{:S(2)}) collective-permute-start(bf16[192,32,128]{2,1,0:T(8,128)(2,1)S(1)} %get-tuple-element.88), channel_id=1, source_target_pairs={{0,32},{4,36},{8,40},{12,44},{16,48},{20,52},{24,56},{28,60},{32,6... | collective-permute-start | bytes 4718600 | tf_op jit(solution)/shard_map/ppermute | solution.py:33
  92.4 27.3 %collective-permute-start.24 = (bf16[64,4096]{1,0:T(8,128)(2,1)S(1)}, bf16[64,4096]{1,0:T(8,128)(2,1)S(1)}, u32[]{:S(2)}, u32[]{:S(2)}) collective-permute-start(bf16[64,4096]{1,0:T(8,128)(2,1)S(1)} %copy-done.15), channel_id=1, source_target_pairs={{0,2},{1,3},{2,0},{3,1},{4,6},{5,7},{6,4},{7,5},{8,10},{9,11},{10,... | collective-permute-start | bytes 1572872 | tf_op jit(solution)/shard_map/ppermute | solution.py:287
  119.7 17.3 %collective-permute-start.23 = (bf16[64,4096]{1,0:T(8,128)(2,1)S(1)}, bf16[64,4096]{1,0:T(8,128)(2,1)}, u32[]{:S(2)}, u32[]{:S(2)}) collective-permute-start(bf16[64,4096]{1,0:T(8,128)(2,1)S(1)} %copy-done.15), channel_id=1, source_target_pairs={{0,1},{1,0},{2,3},{3,2},{4,5},{5,4},{6,7},{7,6},{8,9},{9,8},{10,11... | collective-permute-start | bytes 1572872 | tf_op jit(solution)/shard_map/ppermute | solution.py:287
  119.7 17.3 %collective-permute-start.25 = (bf16[64,4096]{1,0:T(8,128)(2,1)S(1)}, bf16[64,4096]{1,0:T(8,128)(2,1)}, u32[]{:S(2)}, u32[]{:S(2)}) collective-permute-start(bf16[64,4096]{1,0:T(8,128)(2,1)S(1)} %collective-permute-done.24), channel_id=1, source_target_pairs={{0,1},{1,0},{2,3},{3,2},{4,5},{5,4},{6,7},{7,6},{8,9},{9,8},{10,11... | collective-permute-start | bytes 1572872 | tf_op jit(solution)/shard_map/ppermute | solution.py:287
  120.3 16.7 %collective-permute-start.20 = (bf16[64,4096]{1,0:T(8,128)(2,1)S(1)}, bf16[64,4096]{1,0:T(8,128)(2,1)S(1)}, u32[]{:S(2)}, u32[]{:S(2)}) collective-permute-start(bf16[64,4096]{1,0:T(8,128)(2,1)S(1)} %aggregate.1), channel_id=1, source_target_pairs={{0,1},{1,0},{2,3},{3,2},{4,5},{5,4},{6,7},{7,6},{8,9},{9,8},{10,11... | collective-permute-start | bytes 1572872 | tf_op jit(solution)/shard_map/ppermute | solution.py:287
  153.5 38.1 %collective-permute-start.26 = (bf16[192,32,128]{2,1,0:T(8,128)(2,1)S(1)}, bf16[192,32,128]{2,1,0:T(8,128)(2,1)S(1)}, u32[]{:S(2)}, u32[]{:S(2)}) collective-permute-start(bf16[192,32,128]{2,1,0:T(8,128)(2,1)S(1)} %get-tuple-element.91), channel_id=1, source_target_pairs={{0,8},{4,12},{8,16},{12,20},{16,24},{20,28},{24,0},{28,4},{32,40},... | collective-permute-start | bytes 4718600 | tf_op jit(solution)/shard_map/ppermute | solution.py:33
  153.6 38.1 %collective-permute-start.27 = (bf16[192,32,128]{2,1,0:T(8,128)(2,1)S(1)}, bf16[192,32,128]{2,1,0:T(8,128)(2,1)S(1)}, u32[]{:S(2)}, u32[]{:S(2)}) collective-permute-start(bf16[192,32,128]{2,1,0:T(8,128)(2,1)S(1)} %get-tuple-element.92), channel_id=1, source_target_pairs={{0,24},{4,28},{8,0},{12,4},{16,8},{20,12},{24,16},{28,20},{32,56},... | collective-permute-start | bytes 4718600 | tf_op jit(solution)/shard_map/ppermute | solution.py:33
  155.6 37.1 %collective-permute-start.28 = (bf16[192,32,128]{2,1,0:T(8,128)(2,1)S(1)}, bf16[192,32,128]{2,1,0:T(8,128)(2,1)S(1)}, u32[]{:S(2)}, u32[]{:S(2)}) collective-permute-start(bf16[192,32,128]{2,1,0:T(8,128)(2,1)S(1)} %get-tuple-element.93), channel_id=1, source_target_pairs={{0,32},{4,36},{8,40},{12,44},{16,48},{20,52},{24,56},{28,60},{32,6... | collective-permute-start | bytes 4718600 | tf_op jit(solution)/shard_map/ppermute | solution.py:33
  155.9 36.9 %collective-permute-start.29 = (bf16[192,32,128]{2,1,0:T(8,128)(2,1)S(1)}, bf16[192,32,128]{2,1,0:T(8,128)(2,1)S(1)}, u32[]{:S(2)}, u32[]{:S(2)}) collective-permute-start(bf16[192,32,128]{2,1,0:T(8,128)(2,1)S(1)} %get-tuple-element.94), channel_id=1, source_target_pairs={{0,96},{4,100},{8,104},{12,108},{16,112},{20,116},{24,120},{28,124... | collective-permute-start | bytes 4718600 | tf_op jit(solution)/shard_map/ppermute | solution.py:33
  165.3 26.3 %collective-permute-start.31 = (f32[72,256]{1,0:T(8,128)S(1)}, f32[72,256]{1,0:T(8,128)S(1)}, u32[]{:S(2)}, u32[]{:S(2)}) collective-permute-start(f32[72,256]{1,0:T(8,128)S(1)} %fusion.39), channel_id=1, source_target_pairs={{0,8},{4,12},{8,0},{12,4},{16,24},{20,28},{24,16},{28,20},{32,40},... | collective-permute-start | bytes 221192 | tf_op jit(solution)/shard_map/ppermute | solution.py:302
  192.9 17.9 %collective-permute-start.35 = (bf16[64,32,128]{2,1,0:T(8,128)(2,1)S(1)}, bf16[64,32,128]{2,1,0:T(8,128)(2,1)S(1)}, u32[]{:S(2)}, u32[]{:S(2)}) collective-permute-start(bf16[64,32,128]{2,1,0:T(8,128)(2,1)S(1)} %slice.130), channel_id=1, source_target_pairs={{0,96},{4,100},{8,104},{12,108},{16,112},{20,116},{24,120},{28,124... | collective-permute-start | bytes 1572872 | tf_op jit(solution)/shard_map/ppermute | solution.py:33
  195.9 14.9 %collective-permute-start.34 = (bf16[64,32,128]{2,1,0:T(8,128)(2,1)S(1)}, bf16[64,32,128]{2,1,0:T(8,128)(2,1)S(1)}, u32[]{:S(2)}, u32[]{:S(2)}) collective-permute-start(bf16[64,32,128]{2,1,0:T(8,128)(2,1)S(1)} %slice.129), channel_id=1, source_target_pairs={{0,32},{4,36},{8,40},{12,44},{16,48},{20,52},{24,56},{28,60},{32,6... | collective-permute-start | bytes 1572872 | tf_op jit(solution)/shard_map/ppermute | solution.py:33
  195.9 14.9 %collective-permute-start.33 = (bf16[64,32,128]{2,1,0:T(8,128)(2,1)S(1)}, bf16[64,32,128]{2,1,0:T(8,128)(2,1)S(1)}, u32[]{:S(2)}, u32[]{:S(2)}) collective-permute-start(bf16[64,32,128]{2,1,0:T(8,128)(2,1)S(1)} %slice.128), channel_id=1, source_target_pairs={{0,24},{4,28},{8,0},{12,4},{16,8},{20,12},{24,16},{28,20},{32,56},... | collective-permute-start | bytes 1572872 | tf_op jit(solution)/shard_map/ppermute | solution.py:33
  196.2 14.6 %collective-permute-start.32 = (bf16[64,32,128]{2,1,0:T(8,128)(2,1)S(1)}, bf16[64,32,128]{2,1,0:T(8,128)(2,1)S(1)}, u32[]{:S(2)}, u32[]{:S(2)}) collective-permute-start(bf16[64,32,128]{2,1,0:T(8,128)(2,1)S(1)} %slice.127), channel_id=1, source_target_pairs={{0,8},{4,12},{8,16},{12,20},{16,24},{20,28},{24,0},{28,4},{32,40},... | collective-permute-start | bytes 1572872 | tf_op jit(solution)/shard_map/ppermute | solution.py:33
  217.5 15.6 %collective-permute-start.37 = (bf16[32,4096]{1,0:T(8,128)(2,1)S(1)}, bf16[32,4096]{1,0:T(8,128)(2,1)S(1)}, u32[]{:S(2)}, u32[]{:S(2)}) collective-permute-start(bf16[32,4096]{1,0:T(8,128)(2,1)S(1)} %get-tuple-element.112), channel_id=1, source_target_pairs={{0,32},{4,36},{8,40},{12,44},{16,48},{20,52},{24,56},{28,60},{32,6... | collective-permute-start | bytes 786440 | tf_op jit(solution)/shard_map/ppermute | solution.py:33
  217.6 17.1 %collective-permute-start.38 = (bf16[32,4096]{1,0:T(8,128)(2,1)S(1)}, bf16[32,4096]{1,0:T(8,128)(2,1)S(1)}, u32[]{:S(2)}, u32[]{:S(2)}) collective-permute-start(bf16[32,4096]{1,0:T(8,128)(2,1)S(1)} %get-tuple-element.113), channel_id=1, source_target_pairs={{0,64},{4,68},{8,72},{12,76},{16,80},{20,84},{24,88},{28,92},{32,9... | collective-permute-start | bytes 786440 | tf_op jit(solution)/shard_map/ppermute | solution.py:33
  (44 other events, 547.6 us)

commit v2 on v1

--- a/solution.py
+++ b/solution.py
@@ -372,11 +372,11 @@
     parts = row_swap(parts, 0, 2, 0)
     back, parts = lax.optimization_barrier((back, parts))
     folded = fold(asked, back[0] + back[1], width)
-    passed, parts = line_sum(folded, 1).astype(jnp.bfloat16), row_swap(parts, 1, 0, 0)
+    passed, parts = line_sum(folded, 1).astype(jnp.bfloat16), parts
     passed, folded, parts = lax.optimization_barrier((passed, folded, parts))
     arrived = lax.ppermute(passed, "rows", row_perm(0, 0, 1))
     grad_feats = line_sum(folded, 0) + arrived.astype(jnp.float32)
-    parts = row_swap(parts, 2, 0, 0)
+    parts = row_swap(row_swap(parts, 1, 0, 0), 2, 0, 0)
     grad_bias = parts[feat_loc, :feat_loc]
     grad_weight = blocks_by_feat(parts[:feat_loc].T, mine)
     return (activated, grad_feats, grad_weight, grad_bias)

time: 273 us -> 266 us (0.974)
  waiting for transfers between devices: 141 us -> 134 us
    ppermute x1, waiting for transfers between devices: 8.83 us -> 5.45 us  [on_device(): arrived = lax.ppermute(passed, 'rows', row_perm(0, 0, 1))]
  transfers between devices with their start and end apart: 52 -> 52, of which waited for: 23 -> 26; matrix products, arithmetic and copies ran while one was open for 6% -> 6% of each run, Pallas kernels for 6% -> 6%
where the time goes in v2:
time: 266 us; the launch traced here: 265 us
  waiting for transfers between devices  134 us (50%)
  starting transfers between devices  67.4 us (25%)
  Pallas kernels  38.2 us (14%)
  local copies, waits for them, and re-layouts  11.6 us (4%)
  other arithmetic  6.97 us (3%)
  matrix products  5.69 us (2%)
    ppermute x36, waiting for transfers between devices, shift(): lax.ppermute(v, 'rows', row_perm(near, far, 0) if near_axis == 0 else row...  64.7 us
    ppermute x36, starting transfers between devices, shift(): lax.ppermute(v, 'rows', row_perm(near, far, 0) if near_axis == 0 else row...  48.4 us
    ppermute x5, waiting for transfers between devices, row_swap(): return v + lax.ppermute(v, 'rows', pairs)  43.6 us
    pallas_call x1, Pallas kernels, aggregate(): pl.pallas_call(aggregate_kernel, out_shape=jax.ShapeDtypeStruct((2 * half...  15.4 us
    ppermute x9, waiting for transfers between devices, from_feat(): return lax.ppermute(v, 'feat', [(i, i ^ step) for i in range(4)])  12.7 us
    pallas_call x1, Pallas kernels, spread(): pl.pallas_call(spread_kernel, out_shape=[jax.ShapeDtypeStruct((n, half, T...  12.6 us
    ppermute x9, starting transfers between devices, from_feat(): return lax.ppermute(v, 'feat', [(i, i ^ step) for i in range(4)])  10.9 us
    ppermute x1, waiting for transfers between devices, on_device(): other = lax.ppermute(node_feats, 'rows', row_perm(0, 0, 1))  7.94 us
  transfers between devices with their start and end apart: 52, of which 26 were waited for; matrix products, arithmetic and copies ran while one was open for 6% of the time, Pallas kernels for 6%

profile of v2, /device:TPU:24, one launch (start us, length us, event | category | flops | bytes accessed | tf_op | source)
XLA Modules:
  0.0 265.5 jit_solution(9958648967562734469)
XLA Ops:
  6.8 7.9 %collective-permute-done = bf16[64,4096]{1,0:T(8,128)(2,1)S(1)} collective-permute-done((bf16[64,4096]{1,0:T(8,128)(2,1)}, bf16[64,4096]{1,0:T(8,128)(2,1)S(1)}, u32[]{:S(2)}, u32[]{:S(2)}) %collective-permute-start) | collective-permute-done | bytes 524320 | tf_op jit(solution)/shard_map/ppermute | solution.py:318
  20.3 9.2 %collective-permute-done.2.refs_2_ = bf16[64,4224]{1,0:T(8,128)(2,1)S(1)} collective-permute-done((bf16[64,4224]{1,0:T(8,128)(2,1)S(1)}, bf16[64,4224]{1,0:T(8,128)(2,1)S(1)}, u32[]{:S(2)}, u32[]{:S(2)}) %collective-permute-start.2) | collective-permute-done | bytes 540704 | tf_op jit(solution)/shard_map/ppermute | solution.py:33
  44.8 3.5 %pack.1 = (bf16[128,32,128]{2,1,0:T(8,128)(2,1)S(1)}, bf16[192,32,128]{2,1,0:T(8,128)(2,1)S(1)}, bf16[192,32,128]{2,1,0:T(8,128)(2,1)S(1)}, bf16[128,32,128]{2,1...) custom-call(s32[2,4,8,16]{3,2,1,0:T(8,128)S(1)} %pad_add_fusion.asked_ref, ...), custom_call_target="tpu_custom_call" | custom-call | tf_op jit(solution)/shard_map/pack/pallas_call | solution.py:65
  53.7 28.6 %collective-permute-done.12.refs_1_ = bf16[192,32,128]{2,1,0:T(8,128)(2,1)S(1)} collective-permute-done((bf16[192,32,128]{2,1,0:T(8,128)(2,1)S(1)}, bf16[192,32,128]{2,1,0:T(8,128)(2,1)S(1)}, u32[]{:S(2)}, u32[]{:S(2)}) %collective-permute-start.12) | collective-permute-done | bytes 1572896 | tf_op jit(solution)/shard_map/ppermute | solution.py:33
  84.1 3.2 %collective-permute-start.15 = (bf16[64,32,128]{2,1,0:T(8,128)(2,1)}, bf16[64,32,128]{2,1,0:T(8,128)(2,1)S(1)}, u32[]{:S(2)}, u32[]{:S(2)}) collective-permute-start(bf16[64,32,128]{2,1,0:T(8,128)(2,1)} %slice.149), channel_id=1, source_target_pairs={{0,8},{4,12},{8,16},{12,20},{16,24},{20,28},{24,0},{28,4},{32,40},... | collective-permute-start | bytes 1572872 | tf_op jit(solution)/shard_map/ppermute | solution.py:33
  92.4 3.4 %collective-permute-start.24 = (bf16[64,4096]{1,0:T(8,128)(2,1)S(1)}, bf16[64,4096]{1,0:T(8,128)(2,1)S(1)}, u32[]{:S(2)}, u32[]{:S(2)}) collective-permute-start(bf16[64,4096]{1,0:T(8,128)(2,1)S(1)} %copy-done.15), channel_id=1, source_target_pairs={{0,2},{1,3},{2,0},{3,1},{4,6},{5,7},{6,4},{7,5},{8,10},{9,11},{10,... | collective-permute-start | bytes 1572872 | tf_op jit(solution)/shard_map/ppermute | solution.py:287
  97.7 3.3 %collective-permute-done.19.refs_9_ = bf16[64,32,128]{2,1,0:T(8,128)(2,1)} collective-permute-done((bf16[64,32,128]{2,1,0:T(8,128)(2,1)}, bf16[64,32,128]{2,1,0:T(8,128)(2,1)}, u32[]{:S(2)}, u32[]{:S(2)}) %collective-permute-start.19) | collective-permute-done | bytes 524320 | tf_op jit(solution)/shard_map/ppermute | solution.py:33
  101.0 15.4 %aggregate.1 = bf16[64,4096]{1,0:T(8,128)(2,1)S(1)} custom-call(s32[32,16]{1,0:T(8,128)S(1)} %get-tuple-element.155.slot_a_ref, s32[32,16]{1,0:T(8,128)S(1)} %get-tuple-element.154.slot_b_ref, bf16[128,32,128]{2,1,0:T(8,128)(2,1)} %copy-done, bf16[192,32,128]{2,1,0:T(8,128)(2,1)} %copy-done.2, bf16[192,32,128]{2,1,0:T(8,128)(2,1)} %copy-done.3, ...), custom_call_target="tpu_custom_call" | custom-call | tf_op jit(solution)/shard_map/aggregate/pallas_call | solution.py:129
  116.4 3.3 %collective-permute-start.21 = (bf16[64,4096]{1,0:T(8,128)(2,1)S(1)}, bf16[64,4096]{1,0:T(8,128)(2,1)S(1)}, u32[]{:S(2)}, u32[]{:S(2)}) collective-permute-start(bf16[64,4096]{1,0:T(8,128)(2,1)S(1)} %aggregate.1), channel_id=1, source_target_pairs={{0,2},{1,3},{2,0},{3,1},{4,6},{5,7},{6,4},{7,5},{8,10},{9,11},{10,... | collective-permute-start | bytes 1572872 | tf_op jit(solution)/shard_map/ppermute | solution.py:287
  120.4 6.8 %collective-permute-done.21 = bf16[64,4096]{1,0:T(8,128)(2,1)S(1)} collective-permute-done((bf16[64,4096]{1,0:T(8,128)(2,1)S(1)}, bf16[64,4096]{1,0:T(8,128)(2,1)S(1)}, u32[]{:S(2)}, u32[]{:S(2)}) %collective-permute-start.21) | collective-permute-done | bytes 524320 | tf_op jit(solution)/shard_map/ppermute | solution.py:287
  127.2 3.3 %collective-permute-start.10 = (f32[264,64]{0,1:T(8,128)S(1)}, f32[264,64]{0,1:T(8,128)S(1)}, u32[]{:S(2)}, u32[]{:S(2)}) collective-permute-start(f32[264,64]{0,1:T(8,128)S(1)} %pad_maximum_fusion.5), channel_id=1, source_target_pairs={{0,2},{1,3},{2,0},{3,1},{4,6},{5,7},{6,4},{7,5},{8,10},{9,11},{10,... | collective-permute-start | bytes 202760 | tf_op jit(solution)/shard_map/ppermute | solution.py:287
  130.5 3.5 %collective-permute-done.10 = f32[264,64]{0,1:T(8,128)S(1)} collective-permute-done((f32[264,64]{0,1:T(8,128)S(1)}, f32[264,64]{0,1:T(8,128)S(1)}, u32[]{:S(2)}, u32[]{:S(2)}) %collective-permute-start.10) | collective-permute-done | bytes 67616 | tf_op jit(solution)/shard_map/ppermute | solution.py:287
  137.0 3.4 %multiply_convert_fusion = (bf16[256,4096]{1,0:T(8,128)(2,1)S(1)}, f32[256,4096]{1,0:T(8,128)S(1)}, f32[256,4096]{1,0:T(8,128)S(1)}) fusion(bf16[64,4096]{1,0:T(8,128)(2,1)} %collective-permute-done.25, bf16[64,4096]{1,0:T(8,128)(2,1)S(1)} %collective-permute-done.24, bf16[64,4096]{1,0:T(8,128)(2,1)} %collective-permute-done.23, ...), kind=kOutput, calls=%fused_computation.2 | convolution fusion | flops 564658176 | bytes 14812160 | tf_op jit(solution)/shard_map/dot_general | solution.py:355
  140.9 12.6 %spread.1 = (bf16[128,32,128]{2,1,0:T(8,128)(2,1)S(1)}, bf16[192,32,128]{2,1,0:T(8,128)(2,1)S(1)}, bf16[192,32,128]{2,1,0:T(8,128)(2,1)S(1)}, bf16[128,32,128]{2...) custom-call(s32[32,16]{1,0:T(8,128)S(1)} %get-tuple-element.155.slot_a_ref, ...), custom_call_target="tpu_custom_call" | custom-call | tf_op jit(solution)/shard_map/spread/pallas_call | solution.py:179
  155.8 3.0 %collective-permute-start.29 = (bf16[192,32,128]{2,1,0:T(8,128)(2,1)S(1)}, bf16[192,32,128]{2,1,0:T(8,128)(2,1)S(1)}, u32[]{:S(2)}, u32[]{:S(2)}) collective-permute-start(bf16[192,32,128]{2,1,0:T(8,128)(2,1)S(1)} %get-tuple-element.94), channel_id=1, source_target_pairs={{0,96},{4,100},{8,104},{12,108},{16,112},{20,116},{24,120},{28,124... | collective-permute-start | bytes 4718600 | tf_op jit(solution)/shard_map/ppermute | solution.py:33
  162.2 3.1 %collective-permute-done.30 = f32[72,256]{1,0:T(8,128)S(1)} collective-permute-done((f32[72,256]{1,0:T(8,128)S(1)}, f32[72,256]{1,0:T(8,128)S(1)}, u32[]{:S(2)}, u32[]{:S(2)}) %collective-permute-start.30) | collective-permute-done | bytes 73760 | tf_op jit(solution)/shard_map/ppermute | solution.py:302
  165.4 26.2 %collective-permute-done.31 = f32[72,256]{1,0:T(8,128)S(1)} collective-permute-done((f32[72,256]{1,0:T(8,128)S(1)}, f32[72,256]{1,0:T(8,128)S(1)}, u32[]{:S(2)}, u32[]{:S(2)}) %collective-permute-start.31) | collective-permute-done | bytes 73760 | tf_op jit(solution)/shard_map/ppermute | solution.py:302
  192.9 3.0 %collective-permute-start.35 = (bf16[64,32,128]{2,1,0:T(8,128)(2,1)S(1)}, bf16[64,32,128]{2,1,0:T(8,128)(2,1)S(1)}, u32[]{:S(2)}, u32[]{:S(2)}) collective-permute-start(bf16[64,32,128]{2,1,0:T(8,128)(2,1)S(1)} %slice.130), channel_id=1, source_target_pairs={{0,96},{4,100},{8,104},{12,108},{16,112},{20,116},{24,120},{28,124... | collective-permute-start | bytes 1572872 | tf_op jit(solution)/shard_map/ppermute | solution.py:33
  199.2 11.6 %collective-permute-done.36 = f32[72,256]{1,0:T(8,128)S(1)} collective-permute-done((f32[72,256]{1,0:T(8,128)S(1)}, f32[72,256]{1,0:T(8,128)S(1)}, u32[]{:S(2)}, u32[]{:S(2)}) %collective-permute-start.36) | collective-permute-done | bytes 73760 | tf_op jit(solution)/shard_map/ppermute | solution.py:302
  210.8 6.7 %fold.1 = (f32[32,4096]{1,0:T(8,128)S(1)}, bf16[32,4096]{1,0:T(8,128)(2,1)S(1)}, bf16[32,4096]{1,0:T(8,128)(2,1)S(1)}, bf16[32,4096]{1,0:T(8,128)(2,1)S(1)}, f32...) custom-call(s32[2,4,8,16]{3,2,1,0:T(8,128)S(1)} %pad_add_fusion.aske, ...), custom_call_target="tpu_custom_call" | custom-call | tf_op jit(solution)/shard_map/fold/pallas_call | solution.py:238
  217.6 4.3 %collective-permute-start.38 = (bf16[32,4096]{1,0:T(8,128)(2,1)S(1)}, bf16[32,4096]{1,0:T(8,128)(2,1)S(1)}, u32[]{:S(2)}, u32[]{:S(2)}) collective-permute-start(bf16[32,4096]{1,0:T(8,128)(2,1)S(1)} %get-tuple-element.113), channel_id=1, source_target_pairs={{0,64},{4,68},{8,72},{12,76},{16,80},{20,84},{24,88},{28,92},{32,9... | collective-permute-start | bytes 786440 | tf_op jit(solution)/shard_map/ppermute | solution.py:33
  244.0 4.1 %collective-permute-start.44 = (bf16[32,4096]{1,0:T(8,128)(2,1)S(1)}, bf16[32,4096]{1,0:T(8,128)(2,1)S(1)}, u32[]{:S(2)}, u32[]{:S(2)}) collective-permute-start(bf16[32,4096]{1,0:T(8,128)(2,1)S(1)} %get-tuple-element.130), channel_id=1, source_target_pairs={{0,64},{4,68},{8,72},{12,76},{16,80},{20,84},{24,88},{28,92},{32,9... | collective-permute-start | bytes 786440 | tf_op jit(solution)/shard_map/ppermute | solution.py:33
  251.5 3.7 %collective-permute-done.44 = bf16[32,4096]{1,0:T(8,128)(2,1)S(1)} collective-permute-done((bf16[32,4096]{1,0:T(8,128)(2,1)S(1)}, bf16[32,4096]{1,0:T(8,128)(2,1)S(1)}, u32[]{:S(2)}, u32[]{:S(2)}) %collective-permute-start.44) | collective-permute-done | bytes 262176 | tf_op jit(solution)/shard_map/ppermute | solution.py:33
  259.0 5.4 %collective-permute-done.49 = bf16[64,4096]{1,0:T(8,128)(2,1)S(1)} collective-permute-done((bf16[64,4096]{1,0:T(8,128)(2,1)S(1)}, bf16[64,4096]{1,0:T(8,128)(2,1)S(1)}, u32[]{:S(2)}, u32[]{:S(2)}) %collective-permute-start.49) | collective-permute-done | bytes 524320 | tf_op jit(solution)/shard_map/ppermute | solution.py:377
  (197 shorter events, 85.6 us)
Async XLA Ops:
  0.6 14.1 %collective-permute-start = (bf16[64,4096]{1,0:T(8,128)(2,1)}, bf16[64,4096]{1,0:T(8,128)(2,1)S(1)}, u32[]{:S(2)}, u32[]{:S(2)}) collective-permute-start(bf16[64,4096]{1,0:T(8,128)(2,1)} %param.6), channel_id=1, source_target_pairs={{0,4},{4,0},{8,12},{12,8},{16,20},{20,16},{24,28},{28,24},{32,36},... | collective-permute-start | bytes 1572872 | tf_op jit(solution)/shard_map/ppermute | solution.py:318
  14.9 14.6 %collective-permute-start.2 = (bf16[64,4224]{1,0:T(8,128)(2,1)S(1)}, bf16[64,4224]{1,0:T(8,128)(2,1)S(1)}, u32[]{:S(2)}, u32[]{:S(2)}) collective-permute-start(bf16[64,4224]{1,0:T(8,128)(2,1)S(1)} %fusion.4.refs_0_), channel_id=1, source_target_pairs={{0,32},{4,36},{8,40},{12,44},{16,48},{20,52},{24,56},{28,60},{32,6... | collective-permute-start | bytes 1622024 | tf_op jit(solution)/shard_map/ppermute | solution.py:33
  16.4 14.1 %collective-permute-start.1 = (bf16[64,4224]{1,0:T(8,128)(2,1)S(1)}, bf16[64,4224]{1,0:T(8,128)(2,1)S(1)}, u32[]{:S(2)}, u32[]{:S(2)}) collective-permute-start(bf16[64,4224]{1,0:T(8,128)(2,1)S(1)} %fusion.4.refs_0_), channel_id=1, source_target_pairs={{0,96},{4,100},{8,104},{12,108},{16,112},{20,116},{24,120},{28,124... | collective-permute-start | bytes 1622024 | tf_op jit(solution)/shard_map/ppermute | solution.py:33
  18.2 16.0 %collective-permute-start.6 = (bf16[64,4224]{1,0:T(8,128)(2,1)S(1)}, bf16[64,4224]{1,0:T(8,128)(2,1)S(1)}, u32[]{:S(2)}, u32[]{:S(2)}) collective-permute-start(bf16[64,4224]{1,0:T(8,128)(2,1)S(1)} %fusion.5.refs_5_), channel_id=1, source_target_pairs={{0,8},{4,12},{8,16},{12,20},{16,24},{20,28},{24,0},{28,4},{32,40},... | collective-permute-start | bytes 1622024 | tf_op jit(solution)/shard_map/ppermute | solution.py:33
  18.5 16.7 %collective-permute-start.5 = (bf16[64,4224]{1,0:T(8,128)(2,1)S(1)}, bf16[64,4224]{1,0:T(8,128)(2,1)S(1)}, u32[]{:S(2)}, u32[]{:S(2)}) collective-permute-start(bf16[64,4224]{1,0:T(8,128)(2,1)S(1)} %fusion.5.refs_5_), channel_id=1, source_target_pairs={{0,24},{4,28},{8,0},{12,4},{16,8},{20,12},{24,16},{28,20},{32,56},... | collective-permute-start | bytes 1622024 | tf_op jit(solution)/shard_map/ppermute | solution.py:33
  48.3 33.9 %collective-permute-start.12 = (bf16[192,32,128]{2,1,0:T(8,128)(2,1)S(1)}, bf16[192,32,128]{2,1,0:T(8,128)(2,1)S(1)}, u32[]{:S(2)}, u32[]{:S(2)}) collective-permute-start(bf16[192,32,128]{2,1,0:T(8,128)(2,1)S(1)} %get-tuple-element.84), channel_id=1, source_target_pairs={{0,24},{4,28},{8,0},{12,4},{16,8},{20,12},{24,16},{28,20},{32,56},... | collective-permute-start | bytes 4718600 | tf_op jit(solution)/shard_map/ppermute | solution.py:33
  48.9 34.3 %collective-permute-start.13 = (bf16[192,32,128]{2,1,0:T(8,128)(2,1)S(1)}, bf16[192,32,128]{2,1,0:T(8,128)(2,1)S(1)}, u32[]{:S(2)}, u32[]{:S(2)}) collective-permute-start(bf16[192,32,128]{2,1,0:T(8,128)(2,1)S(1)} %get-tuple-element.85), channel_id=1, source_target_pairs={{0,8},{4,12},{8,16},{12,20},{16,24},{20,28},{24,0},{28,4},{32,40},... | collective-permute-start | bytes 4718600 | tf_op jit(solution)/shard_map/ppermute | solution.py:33
  51.6 35.7 %collective-permute-start.16 = (bf16[192,32,128]{2,1,0:T(8,128)(2,1)S(1)}, bf16[192,32,128]{2,1,0:T(8,128)(2,1)S(1)}, u32[]{:S(2)}, u32[]{:S(2)}) collective-permute-start(bf16[192,32,128]{2,1,0:T(8,128)(2,1)S(1)} %get-tuple-element.87), channel_id=1, source_target_pairs={{0,96},{4,100},{8,104},{12,108},{16,112},{20,116},{24,120},{28,124... | collective-permute-start | bytes 4718600 | tf_op jit(solution)/shard_map/ppermute | solution.py:33
  51.9 37.0 %collective-permute-start.17 = (bf16[192,32,128]{2,1,0:T(8,128)(2,1)S(1)}, bf16[192,32,128]{2,1,0:T(8,128)(2,1)S(1)}, u32[]{:S(2)}, u32[]{:S(2)}) collective-permute-start(bf16[192,32,128]{2,1,0:T(8,128)(2,1)S(1)} %get-tuple-element.88), channel_id=1, source_target_pairs={{0,32},{4,36},{8,40},{12,44},{16,48},{20,52},{24,56},{28,60},{32,6... | collective-permute-start | bytes 4718600 | tf_op jit(solution)/shard_map/ppermute | solution.py:33
  83.2 12.7 %collective-permute-start.14 = (bf16[64,32,128]{2,1,0:T(8,128)(2,1)}, bf16[64,32,128]{2,1,0:T(8,128)(2,1)S(1)}, u32[]{:S(2)}, u32[]{:S(2)}) collective-permute-start(bf16[64,32,128]{2,1,0:T(8,128)(2,1)} %slice.148), channel_id=1, source_target_pairs={{0,24},{4,28},{8,0},{12,4},{16,8},{20,12},{24,16},{28,20},{32,56},... | collective-permute-start | bytes 1572872 | tf_op jit(solution)/shard_map/ppermute | solution.py:33
  92.4 27.3 %collective-permute-start.24 = (bf16[64,4096]{1,0:T(8,128)(2,1)S(1)}, bf16[64,4096]{1,0:T(8,128)(2,1)S(1)}, u32[]{:S(2)}, u32[]{:S(2)}) collective-permute-start(bf16[64,4096]{1,0:T(8,128)(2,1)S(1)} %copy-done.15), channel_id=1, source_target_pairs={{0,2},{1,3},{2,0},{3,1},{4,6},{5,7},{6,4},{7,5},{8,10},{9,11},{10,... | collective-permute-start | bytes 1572872 | tf_op jit(solution)/shard_map/ppermute | solution.py:287
  119.7 17.3 %collective-permute-start.23 = (bf16[64,4096]{1,0:T(8,128)(2,1)S(1)}, bf16[64,4096]{1,0:T(8,128)(2,1)}, u32[]{:S(2)}, u32[]{:S(2)}) collective-permute-start(bf16[64,4096]{1,0:T(8,128)(2,1)S(1)} %copy-done.15), channel_id=1, source_target_pairs={{0,1},{1,0},{2,3},{3,2},{4,5},{5,4},{6,7},{7,6},{8,9},{9,8},{10,11... | collective-permute-start | bytes 1572872 | tf_op jit(solution)/shard_map/ppermute | solution.py:287
  119.7 17.3 %collective-permute-start.25 = (bf16[64,4096]{1,0:T(8,128)(2,1)S(1)}, bf16[64,4096]{1,0:T(8,128)(2,1)}, u32[]{:S(2)}, u32[]{:S(2)}) collective-permute-start(bf16[64,4096]{1,0:T(8,128)(2,1)S(1)} %collective-permute-done.24), channel_id=1, source_target_pairs={{0,1},{1,0},{2,3},{3,2},{4,5},{5,4},{6,7},{7,6},{8,9},{9,8},{10,11... | collective-permute-start | bytes 1572872 | tf_op jit(solution)/shard_map/ppermute | solution.py:287
  120.3 16.7 %collective-permute-start.20 = (bf16[64,4096]{1,0:T(8,128)(2,1)S(1)}, bf16[64,4096]{1,0:T(8,128)(2,1)S(1)}, u32[]{:S(2)}, u32[]{:S(2)}) collective-permute-start(bf16[64,4096]{1,0:T(8,128)(2,1)S(1)} %aggregate.1), channel_id=1, source_target_pairs={{0,1},{1,0},{2,3},{3,2},{4,5},{5,4},{6,7},{7,6},{8,9},{9,8},{10,11... | collective-permute-start | bytes 1572872 | tf_op jit(solution)/shard_map/ppermute | solution.py:287
  153.5 38.1 %collective-permute-start.26 = (bf16[192,32,128]{2,1,0:T(8,128)(2,1)S(1)}, bf16[192,32,128]{2,1,0:T(8,128)(2,1)S(1)}, u32[]{:S(2)}, u32[]{:S(2)}) collective-permute-start(bf16[192,32,128]{2,1,0:T(8,128)(2,1)S(1)} %get-tuple-element.91), channel_id=1, source_target_pairs={{0,8},{4,12},{8,16},{12,20},{16,24},{20,28},{24,0},{28,4},{32,40},... | collective-permute-start | bytes 4718600 | tf_op jit(solution)/shard_map/ppermute | solution.py:33
  153.6 38.1 %collective-permute-start.27 = (bf16[192,32,128]{2,1,0:T(8,128)(2,1)S(1)}, bf16[192,32,128]{2,1,0:T(8,128)(2,1)S(1)}, u32[]{:S(2)}, u32[]{:S(2)}) collective-permute-start(bf16[192,32,128]{2,1,0:T(8,128)(2,1)S(1)} %get-tuple-element.92), channel_id=1, source_target_pairs={{0,24},{4,28},{8,0},{12,4},{16,8},{20,12},{24,16},{28,20},{32,56},... | collective-permute-start | bytes 4718600 | tf_op jit(solution)/shard_map/ppermute | solution.py:33
  155.6 37.1 %collective-permute-start.28 = (bf16[192,32,128]{2,1,0:T(8,128)(2,1)S(1)}, bf16[192,32,128]{2,1,0:T(8,128)(2,1)S(1)}, u32[]{:S(2)}, u32[]{:S(2)}) collective-permute-start(bf16[192,32,128]{2,1,0:T(8,128)(2,1)S(1)} %get-tuple-element.93), channel_id=1, source_target_pairs={{0,32},{4,36},{8,40},{12,44},{16,48},{20,52},{24,56},{28,60},{32,6... | collective-permute-start | bytes 4718600 | tf_op jit(solution)/shard_map/ppermute | solution.py:33
  155.8 36.9 %collective-permute-start.29 = (bf16[192,32,128]{2,1,0:T(8,128)(2,1)S(1)}, bf16[192,32,128]{2,1,0:T(8,128)(2,1)S(1)}, u32[]{:S(2)}, u32[]{:S(2)}) collective-permute-start(bf16[192,32,128]{2,1,0:T(8,128)(2,1)S(1)} %get-tuple-element.94), channel_id=1, source_target_pairs={{0,96},{4,100},{8,104},{12,108},{16,112},{20,116},{24,120},{28,124... | collective-permute-start | bytes 4718600 | tf_op jit(solution)/shard_map/ppermute | solution.py:33
  165.3 26.3 %collective-permute-start.31 = (f32[72,256]{1,0:T(8,128)S(1)}, f32[72,256]{1,0:T(8,128)S(1)}, u32[]{:S(2)}, u32[]{:S(2)}) collective-permute-start(f32[72,256]{1,0:T(8,128)S(1)} %fusion.39), channel_id=1, source_target_pairs={{0,8},{4,12},{8,0},{12,4},{16,24},{20,28},{24,16},{28,20},{32,40},... | collective-permute-start | bytes 221192 | tf_op jit(solution)/shard_map/ppermute | solution.py:302
  192.9 17.9 %collective-permute-start.35 = (bf16[64,32,128]{2,1,0:T(8,128)(2,1)S(1)}, bf16[64,32,128]{2,1,0:T(8,128)(2,1)S(1)}, u32[]{:S(2)}, u32[]{:S(2)}) collective-permute-start(bf16[64,32,128]{2,1,0:T(8,128)(2,1)S(1)} %slice.130), channel_id=1, source_target_pairs={{0,96},{4,100},{8,104},{12,108},{16,112},{20,116},{24,120},{28,124... | collective-permute-start | bytes 1572872 | tf_op jit(solution)/shard_map/ppermute | solution.py:33
  195.9 14.9 %collective-permute-start.34 = (bf16[64,32,128]{2,1,0:T(8,128)(2,1)S(1)}, bf16[64,32,128]{2,1,0:T(8,128)(2,1)S(1)}, u32[]{:S(2)}, u32[]{:S(2)}) collective-permute-start(bf16[64,32,128]{2,1,0:T(8,128)(2,1)S(1)} %slice.129), channel_id=1, source_target_pairs={{0,32},{4,36},{8,40},{12,44},{16,48},{20,52},{24,56},{28,60},{32,6... | collective-permute-start | bytes 1572872 | tf_op jit(solution)/shard_map/ppermute | solution.py:33
  195.9 14.9 %collective-permute-start.33 = (bf16[64,32,128]{2,1,0:T(8,128)(2,1)S(1)}, bf16[64,32,128]{2,1,0:T(8,128)(2,1)S(1)}, u32[]{:S(2)}, u32[]{:S(2)}) collective-permute-start(bf16[64,32,128]{2,1,0:T(8,128)(2,1)S(1)} %slice.128), channel_id=1, source_target_pairs={{0,24},{4,28},{8,0},{12,4},{16,8},{20,12},{24,16},{28,20},{32,56},... | collective-permute-start | bytes 1572872 | tf_op jit(solution)/shard_map/ppermute | solution.py:33
  196.2 14.6 %collective-permute-start.32 = (bf16[64,32,128]{2,1,0:T(8,128)(2,1)S(1)}, bf16[64,32,128]{2,1,0:T(8,128)(2,1)S(1)}, u32[]{:S(2)}, u32[]{:S(2)}) collective-permute-start(bf16[64,32,128]{2,1,0:T(8,128)(2,1)S(1)} %slice.127), channel_id=1, source_target_pairs={{0,8},{4,12},{8,16},{12,20},{16,24},{20,28},{24,0},{28,4},{32,40},... | collective-permute-start | bytes 1572872 | tf_op jit(solution)/shard_map/ppermute | solution.py:33
  217.6 13.0 %collective-permute-start.38 = (bf16[32,4096]{1,0:T(8,128)(2,1)S(1)}, bf16[32,4096]{1,0:T(8,128)(2,1)S(1)}, u32[]{:S(2)}, u32[]{:S(2)}) collective-permute-start(bf16[32,4096]{1,0:T(8,128)(2,1)S(1)} %get-tuple-element.113), channel_id=1, source_target_pairs={{0,64},{4,68},{8,72},{12,76},{16,80},{20,84},{24,88},{28,92},{32,9... | collective-permute-start | bytes 786440 | tf_op jit(solution)/shard_map/ppermute | solution.py:33
  (44 other events, 518.9 us)

commit v3 on v2

--- a/solution.py
+++ b/solution.py
@@ -125,7 +125,7 @@
 def aggregate(slot_a, slot_b, got_a, got_b, vals):
     blocks, slots = slot_a.shape
     half = got_a[0].shape[1]
-    per = 4
+    per = 8
     return pl.pallas_call(
         aggregate_kernel,
         out_shape=jax.ShapeDtypeStruct((2 * half, blocks * TB), jnp.bfloat16),
@@ -138,7 +138,7 @@
             scratch_shapes=[pltpu.VMEM((SIDE * PART, half, TB), jnp.bfloat16)] * 2
             + [pltpu.SemaphoreType.DMA((2 * len(LAID),))],
         ),
-        compiler_params=pltpu.CompilerParams(vmem_limit_bytes=16 * MIB),
+        compiler_params=pltpu.CompilerParams(vmem_limit_bytes=22 * MIB),
         name="aggregate",
     )(slot_a, slot_b, *in_hbm(*got_a, *got_b, vals))
 
@@ -175,7 +175,7 @@
 def spread(slot_a, slot_b, mix, vals):
     blocks, slots = slot_a.shape
     half = mix.shape[0] // 2
-    per = 4
+    per = 8
     out = pl.pallas_call(
         spread_kernel,
         out_shape=[jax.ShapeDtypeStruct((n, half, TB), jnp.bfloat16) for n in (PART, PART * 3 // 2, PART * 3 // 2) * 2],
@@ -192,7 +192,7 @@
             ],
             scratch_shapes=[pltpu.VMEM((SIDE * PART, half, TB), jnp.float32)] * 2,
         ),
-        compiler_params=pltpu.CompilerParams(vmem_limit_bytes=34 * MIB),
+        compiler_params=pltpu.CompilerParams(vmem_limit_bytes=40 * MIB),
         name="spread",
     )(slot_a, slot_b, mix, *in_hbm(vals))
     return out[:3], out[3:]

time: 266 us -> 262 us (0.985)
  Pallas kernels: 38.2 us -> 34.5 us
  transfers between devices with their start and end apart: 52 -> 52, of which waited for: 26 -> 26; matrix products, arithmetic and copies ran while one was open for 6% -> 6% of each run, Pallas kernels for 6% -> 5%
where the time goes in v3:
time: 262 us
  waiting for transfers between devices  135 us (52%)
  starting transfers between devices  67.3 us (26%)
  Pallas kernels  34.5 us (13%)
  local copies, waits for them, and re-layouts  11.5 us (4%)
  other arithmetic  7 us (3%)
  matrix products  5.77 us (2%)
    ppermute x36, waiting for transfers between devices, shift(): lax.ppermute(v, 'rows', row_perm(near, far, 0) if near_axis == 0 else row...  64.8 us
    ppermute x36, starting transfers between devices, shift(): lax.ppermute(v, 'rows', row_perm(near, far, 0) if near_axis == 0 else row...  48.3 us
    ppermute x5, waiting for transfers between devices, row_swap(): return v + lax.ppermute(v, 'rows', pairs)  43.7 us
    pallas_call x1, Pallas kernels, aggregate(): pl.pallas_call(aggregate_kernel, out_shape=jax.ShapeDtypeStruct((2 * half...  13.5 us
    ppermute x9, waiting for transfers between devices, from_feat(): return lax.ppermute(v, 'feat', [(i, i ^ step) for i in range(4)])  12.7 us
    ppermute x9, starting transfers between devices, from_feat(): return lax.ppermute(v, 'feat', [(i, i ^ step) for i in range(4)])  10.9 us
    pallas_call x1, Pallas kernels, spread(): pl.pallas_call(spread_kernel, out_shape=[jax.ShapeDtypeStruct((n, half, T...  10.7 us
    ppermute x1, waiting for transfers between devices, on_device(): other = lax.ppermute(node_feats, 'rows', row_perm(0, 0, 1))  7.94 us
  transfers between devices with their start and end apart: 52, of which 26 were waited for; matrix products, arithmetic and copies ran while one was open for 6% of the time, Pallas kernels for 5%

profile of v3, /device:TPU:24, one launch (start us, length us, event | category | flops | bytes accessed | tf_op | source)
XLA Modules:
  0.0 261.9 jit_solution(9735953597326518723)
XLA Ops:
  6.8 7.9 %collective-permute-done = bf16[64,4096]{1,0:T(8,128)(2,1)S(1)} collective-permute-done((bf16[64,4096]{1,0:T(8,128)(2,1)}, bf16[64,4096]{1,0:T(8,128)(2,1)S(1)}, u32[]{:S(2)}, u32[]{:S(2)}) %collective-permute-start) | collective-permute-done | bytes 524320 | tf_op jit(solution)/shard_map/ppermute | solution.py:318
  20.3 9.2 %collective-permute-done.2.refs_2_ = bf16[64,4224]{1,0:T(8,128)(2,1)S(1)} collective-permute-done((bf16[64,4224]{1,0:T(8,128)(2,1)S(1)}, bf16[64,4224]{1,0:T(8,128)(2,1)S(1)}, u32[]{:S(2)}, u32[]{:S(2)}) %collective-permute-start.2) | collective-permute-done | bytes 540704 | tf_op jit(solution)/shard_map/ppermute | solution.py:33
  44.8 3.5 %pack.1 = (bf16[128,32,128]{2,1,0:T(8,128)(2,1)S(1)}, bf16[192,32,128]{2,1,0:T(8,128)(2,1)S(1)}, bf16[192,32,128]{2,1,0:T(8,128)(2,1)S(1)}, bf16[128,32,128]{2,1...) custom-call(s32[2,4,8,16]{3,2,1,0:T(8,128)S(1)} %pad_add_fusion.asked_ref, ...), custom_call_target="tpu_custom_call" | custom-call | tf_op jit(solution)/shard_map/pack/pallas_call | solution.py:65
  53.7 28.6 %collective-permute-done.12.refs_1_ = bf16[192,32,128]{2,1,0:T(8,128)(2,1)S(1)} collective-permute-done((bf16[192,32,128]{2,1,0:T(8,128)(2,1)S(1)}, bf16[192,32,128]{2,1,0:T(8,128)(2,1)S(1)}, u32[]{:S(2)}, u32[]{:S(2)}) %collective-permute-start.12) | collective-permute-done | bytes 1572896 | tf_op jit(solution)/shard_map/ppermute | solution.py:33
  84.1 3.2 %collective-permute-start.15 = (bf16[64,32,128]{2,1,0:T(8,128)(2,1)}, bf16[64,32,128]{2,1,0:T(8,128)(2,1)S(1)}, u32[]{:S(2)}, u32[]{:S(2)}) collective-permute-start(bf16[64,32,128]{2,1,0:T(8,128)(2,1)} %slice.149), channel_id=1, source_target_pairs={{0,8},{4,12},{8,16},{12,20},{16,24},{20,28},{24,0},{28,4},{32,40},... | collective-permute-start | bytes 1572872 | tf_op jit(solution)/shard_map/ppermute | solution.py:33
  92.3 3.4 %collective-permute-start.24 = (bf16[64,4096]{1,0:T(8,128)(2,1)}, bf16[64,4096]{1,0:T(8,128)(2,1)}, u32[]{:S(2)}, u32[]{:S(2)}) collective-permute-start(bf16[64,4096]{1,0:T(8,128)(2,1)} %param.11), channel_id=1, source_target_pairs={{0,2},{1,3},{2,0},{3,1},{4,6},{5,7},{6,4},{7,5},{8,10},{9,11},{10,... | collective-permute-start | bytes 1572872 | tf_op jit(solution)/shard_map/ppermute | solution.py:287
  97.7 3.3 %collective-permute-done.19.refs_9_ = bf16[64,32,128]{2,1,0:T(8,128)(2,1)} collective-permute-done((bf16[64,32,128]{2,1,0:T(8,128)(2,1)}, bf16[64,32,128]{2,1,0:T(8,128)(2,1)}, u32[]{:S(2)}, u32[]{:S(2)}) %collective-permute-start.19) | collective-permute-done | bytes 524320 | tf_op jit(solution)/shard_map/ppermute | solution.py:33
  101.0 13.5 %aggregate.1 = bf16[64,4096]{1,0:T(8,128)(2,1)S(1)} custom-call(s32[32,16]{1,0:T(8,128)S(1)} %get-tuple-element.155.slot_a_ref, s32[32,16]{1,0:T(8,128)S(1)} %get-tuple-element.154.slot_b_ref, bf16[128,32,128]{2,1,0:T(8,128)(2,1)} %copy-done, bf16[192,32,128]{2,1,0:T(8,128)(2,1)} %copy-done.2, bf16[192,32,128]{2,1,0:T(8,128)(2,1)} %copy-done.3, ...), custom_call_target="tpu_custom_call" | custom-call | tf_op jit(solution)/shard_map/aggregate/pallas_call | solution.py:129
  114.5 3.3 %collective-permute-start.21 = (bf16[64,4096]{1,0:T(8,128)(2,1)S(1)}, bf16[64,4096]{1,0:T(8,128)(2,1)S(1)}, u32[]{:S(2)}, u32[]{:S(2)}) collective-permute-start(bf16[64,4096]{1,0:T(8,128)(2,1)S(1)} %aggregate.1), channel_id=1, source_target_pairs={{0,2},{1,3},{2,0},{3,1},{4,6},{5,7},{6,4},{7,5},{8,10},{9,11},{10,... | collective-permute-start | bytes 1572872 | tf_op jit(solution)/shard_map/ppermute | solution.py:287
  118.5 6.8 %collective-permute-done.21 = bf16[64,4096]{1,0:T(8,128)(2,1)S(1)} collective-permute-done((bf16[64,4096]{1,0:T(8,128)(2,1)S(1)}, bf16[64,4096]{1,0:T(8,128)(2,1)S(1)}, u32[]{:S(2)}, u32[]{:S(2)}) %collective-permute-start.21) | collective-permute-done | bytes 524320 | tf_op jit(solution)/shard_map/ppermute | solution.py:287
  125.3 3.3 %collective-permute-start.10 = (f32[264,64]{0,1:T(8,128)S(1)}, f32[264,64]{0,1:T(8,128)S(1)}, u32[]{:S(2)}, u32[]{:S(2)}) collective-permute-start(f32[264,64]{0,1:T(8,128)S(1)} %pad_maximum_fusion.5), channel_id=1, source_target_pairs={{0,2},{1,3},{2,0},{3,1},{4,6},{5,7},{6,4},{7,5},{8,10},{9,11},{10,... | collective-permute-start | bytes 202760 | tf_op jit(solution)/shard_map/ppermute | solution.py:287
  128.6 3.5 %collective-permute-done.10 = f32[264,64]{0,1:T(8,128)S(1)} collective-permute-done((f32[264,64]{0,1:T(8,128)S(1)}, f32[264,64]{0,1:T(8,128)S(1)}, u32[]{:S(2)}, u32[]{:S(2)}) %collective-permute-start.10) | collective-permute-done | bytes 67616 | tf_op jit(solution)/shard_map/ppermute | solution.py:287
  135.1 3.5 %multiply_convert_fusion = (bf16[256,4096]{1,0:T(8,128)(2,1)S(1)}, f32[256,4096]{1,0:T(8,128)S(1)}, f32[256,4096]{1,0:T(8,128)S(1)}) fusion(bf16[64,4096]{1,0:T(8,128)(2,1)} %collective-permute-done.25, bf16[64,4096]{1,0:T(8,128)(2,1)} %collective-permute-done.24, bf16[64,4096]{1,0:T(8,128)(2,1)} %collective-permute-done.23, ...), kind=kOutput, calls=%fused_computation.2 | convolution fusion | flops 564658176 | bytes 14812160 | tf_op jit(solution)/shard_map/dot_general | solution.py:355
  139.1 10.7 %spread.1 = (bf16[128,32,128]{2,1,0:T(8,128)(2,1)S(1)}, bf16[192,32,128]{2,1,0:T(8,128)(2,1)S(1)}, bf16[192,32,128]{2,1,0:T(8,128)(2,1)S(1)}, bf16[128,32,128]{2...) custom-call(s32[32,16]{1,0:T(8,128)S(1)} %get-tuple-element.155.slot_a_ref, ...), custom_call_target="tpu_custom_call" | custom-call | tf_op jit(solution)/shard_map/spread/pallas_call | solution.py:179
  152.2 3.0 %collective-permute-start.29 = (bf16[192,32,128]{2,1,0:T(8,128)(2,1)S(1)}, bf16[192,32,128]{2,1,0:T(8,128)(2,1)S(1)}, u32[]{:S(2)}, u32[]{:S(2)}) collective-permute-start(bf16[192,32,128]{2,1,0:T(8,128)(2,1)S(1)} %get-tuple-element.94), channel_id=1, source_target_pairs={{0,96},{4,100},{8,104},{12,108},{16,112},{20,116},{24,120},{28,124... | collective-permute-start | bytes 4718600 | tf_op jit(solution)/shard_map/ppermute | solution.py:33
  158.5 3.1 %collective-permute-done.30 = f32[72,256]{1,0:T(8,128)S(1)} collective-permute-done((f32[72,256]{1,0:T(8,128)S(1)}, f32[72,256]{1,0:T(8,128)S(1)}, u32[]{:S(2)}, u32[]{:S(2)}) %collective-permute-start.30) | collective-permute-done | bytes 73760 | tf_op jit(solution)/shard_map/ppermute | solution.py:302
  161.7 26.2 %collective-permute-done.31 = f32[72,256]{1,0:T(8,128)S(1)} collective-permute-done((f32[72,256]{1,0:T(8,128)S(1)}, f32[72,256]{1,0:T(8,128)S(1)}, u32[]{:S(2)}, u32[]{:S(2)}) %collective-permute-start.31) | collective-permute-done | bytes 73760 | tf_op jit(solution)/shard_map/ppermute | solution.py:302
  189.2 3.0 %collective-permute-start.35 = (bf16[64,32,128]{2,1,0:T(8,128)(2,1)S(1)}, bf16[64,32,128]{2,1,0:T(8,128)(2,1)S(1)}, u32[]{:S(2)}, u32[]{:S(2)}) collective-permute-start(bf16[64,32,128]{2,1,0:T(8,128)(2,1)S(1)} %slice.130), channel_id=1, source_target_pairs={{0,96},{4,100},{8,104},{12,108},{16,112},{20,116},{24,120},{28,124... | collective-permute-start | bytes 1572872 | tf_op jit(solution)/shard_map/ppermute | solution.py:33
  195.5 11.6 %collective-permute-done.36 = f32[72,256]{1,0:T(8,128)S(1)} collective-permute-done((f32[72,256]{1,0:T(8,128)S(1)}, f32[72,256]{1,0:T(8,128)S(1)}, u32[]{:S(2)}, u32[]{:S(2)}) %collective-permute-start.36) | collective-permute-done | bytes 73760 | tf_op jit(solution)/shard_map/ppermute | solution.py:302
  207.2 6.7 %fold.1 = (f32[32,4096]{1,0:T(8,128)S(1)}, bf16[32,4096]{1,0:T(8,128)(2,1)S(1)}, bf16[32,4096]{1,0:T(8,128)(2,1)S(1)}, bf16[32,4096]{1,0:T(8,128)(2,1)S(1)}, f32...) custom-call(s32[2,4,8,16]{3,2,1,0:T(8,128)S(1)} %pad_add_fusion.aske, ...), custom_call_target="tpu_custom_call" | custom-call | tf_op jit(solution)/shard_map/fold/pallas_call | solution.py:238
  214.0 4.4 %collective-permute-start.38 = (bf16[32,4096]{1,0:T(8,128)(2,1)S(1)}, bf16[32,4096]{1,0:T(8,128)(2,1)S(1)}, u32[]{:S(2)}, u32[]{:S(2)}) collective-permute-start(bf16[32,4096]{1,0:T(8,128)(2,1)S(1)} %get-tuple-element.113), channel_id=1, source_target_pairs={{0,64},{4,68},{8,72},{12,76},{16,80},{20,84},{24,88},{28,92},{32,9... | collective-permute-start | bytes 786440 | tf_op jit(solution)/shard_map/ppermute | solution.py:33
  240.3 4.1 %collective-permute-start.44 = (bf16[32,4096]{1,0:T(8,128)(2,1)S(1)}, bf16[32,4096]{1,0:T(8,128)(2,1)S(1)}, u32[]{:S(2)}, u32[]{:S(2)}) collective-permute-start(bf16[32,4096]{1,0:T(8,128)(2,1)S(1)} %get-tuple-element.130), channel_id=1, source_target_pairs={{0,64},{4,68},{8,72},{12,76},{16,80},{20,84},{24,88},{28,92},{32,9... | collective-permute-start | bytes 786440 | tf_op jit(solution)/shard_map/ppermute | solution.py:33
  247.9 3.7 %collective-permute-done.44 = bf16[32,4096]{1,0:T(8,128)(2,1)S(1)} collective-permute-done((bf16[32,4096]{1,0:T(8,128)(2,1)S(1)}, bf16[32,4096]{1,0:T(8,128)(2,1)S(1)}, u32[]{:S(2)}, u32[]{:S(2)}) %collective-permute-start.44) | collective-permute-done | bytes 262176 | tf_op jit(solution)/shard_map/ppermute | solution.py:33
  255.4 5.4 %collective-permute-done.49 = bf16[64,4096]{1,0:T(8,128)(2,1)S(1)} collective-permute-done((bf16[64,4096]{1,0:T(8,128)(2,1)S(1)}, bf16[64,4096]{1,0:T(8,128)(2,1)S(1)}, u32[]{:S(2)}, u32[]{:S(2)}) %collective-permute-start.49) | collective-permute-done | bytes 524320 | tf_op jit(solution)/shard_map/ppermute | solution.py:377
  (197 shorter events, 85.6 us)
Async XLA Ops:
  0.6 14.1 %collective-permute-start = (bf16[64,4096]{1,0:T(8,128)(2,1)}, bf16[64,4096]{1,0:T(8,128)(2,1)S(1)}, u32[]{:S(2)}, u32[]{:S(2)}) collective-permute-start(bf16[64,4096]{1,0:T(8,128)(2,1)} %param.6), channel_id=1, source_target_pairs={{0,4},{4,0},{8,12},{12,8},{16,20},{20,16},{24,28},{28,24},{32,36},... | collective-permute-start | bytes 1572872 | tf_op jit(solution)/shard_map/ppermute | solution.py:318
  14.9 14.6 %collective-permute-start.2 = (bf16[64,4224]{1,0:T(8,128)(2,1)S(1)}, bf16[64,4224]{1,0:T(8,128)(2,1)S(1)}, u32[]{:S(2)}, u32[]{:S(2)}) collective-permute-start(bf16[64,4224]{1,0:T(8,128)(2,1)S(1)} %fusion.4.refs_0_), channel_id=1, source_target_pairs={{0,32},{4,36},{8,40},{12,44},{16,48},{20,52},{24,56},{28,60},{32,6... | collective-permute-start | bytes 1622024 | tf_op jit(solution)/shard_map/ppermute | solution.py:33
  16.4 14.1 %collective-permute-start.1 = (bf16[64,4224]{1,0:T(8,128)(2,1)S(1)}, bf16[64,4224]{1,0:T(8,128)(2,1)S(1)}, u32[]{:S(2)}, u32[]{:S(2)}) collective-permute-start(bf16[64,4224]{1,0:T(8,128)(2,1)S(1)} %fusion.4.refs_0_), channel_id=1, source_target_pairs={{0,96},{4,100},{8,104},{12,108},{16,112},{20,116},{24,120},{28,124... | collective-permute-start | bytes 1622024 | tf_op jit(solution)/shard_map/ppermute | solution.py:33
  18.2 16.0 %collective-permute-start.6 = (bf16[64,4224]{1,0:T(8,128)(2,1)S(1)}, bf16[64,4224]{1,0:T(8,128)(2,1)S(1)}, u32[]{:S(2)}, u32[]{:S(2)}) collective-permute-start(bf16[64,4224]{1,0:T(8,128)(2,1)S(1)} %fusion.5.refs_5_), channel_id=1, source_target_pairs={{0,8},{4,12},{8,16},{12,20},{16,24},{20,28},{24,0},{28,4},{32,40},... | collective-permute-start | bytes 1622024 | tf_op jit(solution)/shard_map/ppermute | solution.py:33
  18.5 16.7 %collective-permute-start.5 = (bf16[64,4224]{1,0:T(8,128)(2,1)S(1)}, bf16[64,4224]{1,0:T(8,128)(2,1)S(1)}, u32[]{:S(2)}, u32[]{:S(2)}) collective-permute-start(bf16[64,4224]{1,0:T(8,128)(2,1)S(1)} %fusion.5.refs_5_), channel_id=1, source_target_pairs={{0,24},{4,28},{8,0},{12,4},{16,8},{20,12},{24,16},{28,20},{32,56},... | collective-permute-start | bytes 1622024 | tf_op jit(solution)/shard_map/ppermute | solution.py:33
  48.3 33.9 %collective-permute-start.12 = (bf16[192,32,128]{2,1,0:T(8,128)(2,1)S(1)}, bf16[192,32,128]{2,1,0:T(8,128)(2,1)S(1)}, u32[]{:S(2)}, u32[]{:S(2)}) collective-permute-start(bf16[192,32,128]{2,1,0:T(8,128)(2,1)S(1)} %get-tuple-element.84), channel_id=1, source_target_pairs={{0,24},{4,28},{8,0},{12,4},{16,8},{20,12},{24,16},{28,20},{32,56},... | collective-permute-start | bytes 4718600 | tf_op jit(solution)/shard_map/ppermute | solution.py:33
  48.9 34.3 %collective-permute-start.13 = (bf16[192,32,128]{2,1,0:T(8,128)(2,1)S(1)}, bf16[192,32,128]{2,1,0:T(8,128)(2,1)S(1)}, u32[]{:S(2)}, u32[]{:S(2)}) collective-permute-start(bf16[192,32,128]{2,1,0:T(8,128)(2,1)S(1)} %get-tuple-element.85), channel_id=1, source_target_pairs={{0,8},{4,12},{8,16},{12,20},{16,24},{20,28},{24,0},{28,4},{32,40},... | collective-permute-start | bytes 4718600 | tf_op jit(solution)/shard_map/ppermute | solution.py:33
  51.6 35.7 %collective-permute-start.16 = (bf16[192,32,128]{2,1,0:T(8,128)(2,1)S(1)}, bf16[192,32,128]{2,1,0:T(8,128)(2,1)S(1)}, u32[]{:S(2)}, u32[]{:S(2)}) collective-permute-start(bf16[192,32,128]{2,1,0:T(8,128)(2,1)S(1)} %get-tuple-element.87), channel_id=1, source_target_pairs={{0,96},{4,100},{8,104},{12,108},{16,112},{20,116},{24,120},{28,124... | collective-permute-start | bytes 4718600 | tf_op jit(solution)/shard_map/ppermute | solution.py:33
  51.9 37.0 %collective-permute-start.17 = (bf16[192,32,128]{2,1,0:T(8,128)(2,1)S(1)}, bf16[192,32,128]{2,1,0:T(8,128)(2,1)S(1)}, u32[]{:S(2)}, u32[]{:S(2)}) collective-permute-start(bf16[192,32,128]{2,1,0:T(8,128)(2,1)S(1)} %get-tuple-element.88), channel_id=1, source_target_pairs={{0,32},{4,36},{8,40},{12,44},{16,48},{20,52},{24,56},{28,60},{32,6... | collective-permute-start | bytes 4718600 | tf_op jit(solution)/shard_map/ppermute | solution.py:33
  83.2 12.6 %collective-permute-start.14 = (bf16[64,32,128]{2,1,0:T(8,128)(2,1)}, bf16[64,32,128]{2,1,0:T(8,128)(2,1)S(1)}, u32[]{:S(2)}, u32[]{:S(2)}) collective-permute-start(bf16[64,32,128]{2,1,0:T(8,128)(2,1)} %slice.148), channel_id=1, source_target_pairs={{0,24},{4,28},{8,0},{12,4},{16,8},{20,12},{24,16},{28,20},{32,56},... | collective-permute-start | bytes 1572872 | tf_op jit(solution)/shard_map/ppermute | solution.py:33
  92.3 25.5 %collective-permute-start.24 = (bf16[64,4096]{1,0:T(8,128)(2,1)}, bf16[64,4096]{1,0:T(8,128)(2,1)}, u32[]{:S(2)}, u32[]{:S(2)}) collective-permute-start(bf16[64,4096]{1,0:T(8,128)(2,1)} %param.11), channel_id=1, source_target_pairs={{0,2},{1,3},{2,0},{3,1},{4,6},{5,7},{6,4},{7,5},{8,10},{9,11},{10,... | collective-permute-start | bytes 1572872 | tf_op jit(solution)/shard_map/ppermute | solution.py:287
  117.8 17.3 %collective-permute-start.23 = (bf16[64,4096]{1,0:T(8,128)(2,1)S(1)}, bf16[64,4096]{1,0:T(8,128)(2,1)}, u32[]{:S(2)}, u32[]{:S(2)}) collective-permute-start(bf16[64,4096]{1,0:T(8,128)(2,1)S(1)} %copy-done.15), channel_id=1, source_target_pairs={{0,1},{1,0},{2,3},{3,2},{4,5},{5,4},{6,7},{7,6},{8,9},{9,8},{10,11... | collective-permute-start | bytes 1572872 | tf_op jit(solution)/shard_map/ppermute | solution.py:287
  117.8 17.3 %collective-permute-start.25 = (bf16[64,4096]{1,0:T(8,128)(2,1)}, bf16[64,4096]{1,0:T(8,128)(2,1)}, u32[]{:S(2)}, u32[]{:S(2)}) collective-permute-start(bf16[64,4096]{1,0:T(8,128)(2,1)} %collective-permute-done.24), channel_id=1, source_target_pairs={{0,1},{1,0},{2,3},{3,2},{4,5},{5,4},{6,7},{7,6},{8,9},{9,8},{10,11... | collective-permute-start | bytes 1572872 | tf_op jit(solution)/shard_map/ppermute | solution.py:287
  118.4 16.7 %collective-permute-start.20 = (bf16[64,4096]{1,0:T(8,128)(2,1)S(1)}, bf16[64,4096]{1,0:T(8,128)(2,1)S(1)}, u32[]{:S(2)}, u32[]{:S(2)}) collective-permute-start(bf16[64,4096]{1,0:T(8,128)(2,1)S(1)} %aggregate.1), channel_id=1, source_target_pairs={{0,1},{1,0},{2,3},{3,2},{4,5},{5,4},{6,7},{7,6},{8,9},{9,8},{10,11... | collective-permute-start | bytes 1572872 | tf_op jit(solution)/shard_map/ppermute | solution.py:287
  149.8 38.1 %collective-permute-start.26 = (bf16[192,32,128]{2,1,0:T(8,128)(2,1)S(1)}, bf16[192,32,128]{2,1,0:T(8,128)(2,1)S(1)}, u32[]{:S(2)}, u32[]{:S(2)}) collective-permute-start(bf16[192,32,128]{2,1,0:T(8,128)(2,1)S(1)} %get-tuple-element.91), channel_id=1, source_target_pairs={{0,8},{4,12},{8,16},{12,20},{16,24},{20,28},{24,0},{28,4},{32,40},... | collective-permute-start | bytes 4718600 | tf_op jit(solution)/shard_map/ppermute | solution.py:33
  149.9 38.1 %collective-permute-start.27 = (bf16[192,32,128]{2,1,0:T(8,128)(2,1)S(1)}, bf16[192,32,128]{2,1,0:T(8,128)(2,1)S(1)}, u32[]{:S(2)}, u32[]{:S(2)}) collective-permute-start(bf16[192,32,128]{2,1,0:T(8,128)(2,1)S(1)} %get-tuple-element.92), channel_id=1, source_target_pairs={{0,24},{4,28},{8,0},{12,4},{16,8},{20,12},{24,16},{28,20},{32,56},... | collective-permute-start | bytes 4718600 | tf_op jit(solution)/shard_map/ppermute | solution.py:33
  151.9 37.1 %collective-permute-start.28 = (bf16[192,32,128]{2,1,0:T(8,128)(2,1)S(1)}, bf16[192,32,128]{2,1,0:T(8,128)(2,1)S(1)}, u32[]{:S(2)}, u32[]{:S(2)}) collective-permute-start(bf16[192,32,128]{2,1,0:T(8,128)(2,1)S(1)} %get-tuple-element.93), channel_id=1, source_target_pairs={{0,32},{4,36},{8,40},{12,44},{16,48},{20,52},{24,56},{28,60},{32,6... | collective-permute-start | bytes 4718600 | tf_op jit(solution)/shard_map/ppermute | solution.py:33
  152.2 36.9 %collective-permute-start.29 = (bf16[192,32,128]{2,1,0:T(8,128)(2,1)S(1)}, bf16[192,32,128]{2,1,0:T(8,128)(2,1)S(1)}, u32[]{:S(2)}, u32[]{:S(2)}) collective-permute-start(bf16[192,32,128]{2,1,0:T(8,128)(2,1)S(1)} %get-tuple-element.94), channel_id=1, source_target_pairs={{0,96},{4,100},{8,104},{12,108},{16,112},{20,116},{24,120},{28,124... | collective-permute-start | bytes 4718600 | tf_op jit(solution)/shard_map/ppermute | solution.py:33
  161.6 26.3 %collective-permute-start.31 = (f32[72,256]{1,0:T(8,128)S(1)}, f32[72,256]{1,0:T(8,128)S(1)}, u32[]{:S(2)}, u32[]{:S(2)}) collective-permute-start(f32[72,256]{1,0:T(8,128)S(1)} %fusion.39), channel_id=1, source_target_pairs={{0,8},{4,12},{8,0},{12,4},{16,24},{20,28},{24,16},{28,20},{32,40},... | collective-permute-start | bytes 221192 | tf_op jit(solution)/shard_map/ppermute | solution.py:302
  189.2 17.9 %collective-permute-start.35 = (bf16[64,32,128]{2,1,0:T(8,128)(2,1)S(1)}, bf16[64,32,128]{2,1,0:T(8,128)(2,1)S(1)}, u32[]{:S(2)}, u32[]{:S(2)}) collective-permute-start(bf16[64,32,128]{2,1,0:T(8,128)(2,1)S(1)} %slice.130), channel_id=1, source_target_pairs={{0,96},{4,100},{8,104},{12,108},{16,112},{20,116},{24,120},{28,124... | collective-permute-start | bytes 1572872 | tf_op jit(solution)/shard_map/ppermute | solution.py:33
  192.2 14.9 %collective-permute-start.34 = (bf16[64,32,128]{2,1,0:T(8,128)(2,1)S(1)}, bf16[64,32,128]{2,1,0:T(8,128)(2,1)S(1)}, u32[]{:S(2)}, u32[]{:S(2)}) collective-permute-start(bf16[64,32,128]{2,1,0:T(8,128)(2,1)S(1)} %slice.129), channel_id=1, source_target_pairs={{0,32},{4,36},{8,40},{12,44},{16,48},{20,52},{24,56},{28,60},{32,6... | collective-permute-start | bytes 1572872 | tf_op jit(solution)/shard_map/ppermute | solution.py:33
  192.2 14.9 %collective-permute-start.33 = (bf16[64,32,128]{2,1,0:T(8,128)(2,1)S(1)}, bf16[64,32,128]{2,1,0:T(8,128)(2,1)S(1)}, u32[]{:S(2)}, u32[]{:S(2)}) collective-permute-start(bf16[64,32,128]{2,1,0:T(8,128)(2,1)S(1)} %slice.128), channel_id=1, source_target_pairs={{0,24},{4,28},{8,0},{12,4},{16,8},{20,12},{24,16},{28,20},{32,56},... | collective-permute-start | bytes 1572872 | tf_op jit(solution)/shard_map/ppermute | solution.py:33
  192.5 14.6 %collective-permute-start.32 = (bf16[64,32,128]{2,1,0:T(8,128)(2,1)S(1)}, bf16[64,32,128]{2,1,0:T(8,128)(2,1)S(1)}, u32[]{:S(2)}, u32[]{:S(2)}) collective-permute-start(bf16[64,32,128]{2,1,0:T(8,128)(2,1)S(1)} %slice.127), channel_id=1, source_target_pairs={{0,8},{4,12},{8,16},{12,20},{16,24},{20,28},{24,0},{28,4},{32,40},... | collective-permute-start | bytes 1572872 | tf_op jit(solution)/shard_map/ppermute | solution.py:33
  214.0 13.2 %collective-permute-start.38 = (bf16[32,4096]{1,0:T(8,128)(2,1)S(1)}, bf16[32,4096]{1,0:T(8,128)(2,1)S(1)}, u32[]{:S(2)}, u32[]{:S(2)}) collective-permute-start(bf16[32,4096]{1,0:T(8,128)(2,1)S(1)} %get-tuple-element.113), channel_id=1, source_target_pairs={{0,64},{4,68},{8,72},{12,76},{16,80},{20,84},{24,88},{28,92},{32,9... | collective-permute-start | bytes 786440 | tf_op jit(solution)/shard_map/ppermute | solution.py:33
  (44 other events, 491.3 us)
